TPU v7x, 512 devices: a whole 4x8x8 slice. The times are simulated.
512 devices in a mesh: dp: 32 (over x, y), ctx: 16 (over z, core).
Axes of the slice: x: 4, y: 8, z: 8, core: 2. Of those that a mesh axis runs over, the one named last changes fastest.
Arguments:
- keys_a: bfloat16 [32, 2048, 2560], P('dp', 'ctx'), may hold values from -6 to 6
- values_a: bfloat16 [32, 2048, 2560], P('dp', 'ctx'), may hold values from -6 to 6
- queries_b: bfloat16 [32, 2048, 2560], P('dp', 'ctx'), may hold values from -6 to 6
- grad_out: bfloat16 [32, 2048, 2560], P('dp', 'ctx'), may hold values from -1.5 to 1.5
- state_start: float32 [3, 20, 128, 128], P(None, None, 'ctx'), may hold values from -0.5 to 0.5
- state_next: float32 [32, 3, 20, 128, 128], P('dp', None, None, 'ctx'), may hold values from -0.5 to 0.5
Outputs:
- grad_keys: bfloat16 [32, 2048, 2560], P('dp', 'ctx')
- grad_values: bfloat16 [32, 2048, 2560], P('dp', 'ctx')
- grad_state: float32 [3, 20, 128, 128], P(None, None, 'ctx')
All inputs are finite; a program needn't handle non-finite values.
Results may differ from a plain program's by a relative error of at most 0.033.
Values may be sent and summed in bfloat16 or wider, within the bound.
A program may use at most 128 MiB of HBM per device.

v0:
```python
import jax
import jax.numpy as jnp
from jax import lax
from jax.sharding import PartitionSpec as P

D = 128
H = 20
F = 128
NS_STEPS = 2


step_rate = 4.0
coef_a = 3.4445
coef_b = -4.775
coef_c = 2.0315


def sent_together(arrays, axis, split_dim, concat_dim, along):
    widths = [a.shape[along] for a in arrays]
    both = jnp.concatenate(arrays, axis=along)
    out = lax.all_to_all(both, axis, split_axis=split_dim, concat_axis=concat_dim, tiled=True)
    return tuple(jnp.split(out, [sum(widths[:k]) for k in range(1, len(widths))], axis=along))


def gathered_total(shard, axis):
    parts = lax.all_gather(shard, axis).astype(jnp.float32)
    return parts.sum(axis=0)


def field_grad(weights, inputs, targets):
    gate_pre = jnp.einsum("thd,hdf->thf", inputs, weights[0], preferred_element_type=jnp.float32)
    up_pre = jnp.einsum("thd,hdf->thf", inputs, weights[1], preferred_element_type=jnp.float32)
    target_proj = jnp.einsum(
        "thd,hdf->thf", targets, weights[2], preferred_element_type=jnp.float32
    )
    sigmoid_val = jax.nn.sigmoid(gate_pre)
    swish_val = gate_pre * sigmoid_val
    hidden = (swish_val * up_pre).astype(jnp.bfloat16)
    d_gate = (target_proj * up_pre * sigmoid_val * (1.0 + gate_pre * (1.0 - sigmoid_val))).astype(
        jnp.bfloat16
    )
    d_up = (target_proj * swish_val).astype(jnp.bfloat16)
    grad_a = jnp.einsum("thd,thf->hdf", inputs, d_gate, preferred_element_type=jnp.float32)
    grad_b = jnp.einsum("thd,thf->hdf", inputs, d_up, preferred_element_type=jnp.float32)
    grad_c = jnp.einsum("thd,thf->hdf", targets, hidden, preferred_element_type=jnp.float32)
    return jnp.stack([grad_a, grad_b, grad_c])


def newton(gradients):
    scale_norm = jnp.sqrt(jnp.sum(gradients * gradients, axis=(1, 2), keepdims=True) + 1e-06)
    iterate = (gradients / scale_norm).astype(jnp.bfloat16)
    for repeat in range(NS_STEPS):
        gram_block = jnp.einsum(
            "mdf,mef->mde", iterate, iterate, preferred_element_type=jnp.float32
        ).astype(jnp.bfloat16)
        square = jnp.einsum(
            "mde,mek->mdk", gram_block, gram_block, preferred_element_type=jnp.float32
        )
        poly_term = (coef_b * gram_block.astype(jnp.float32) + coef_c * square).astype(jnp.bfloat16)
        mixed = jnp.einsum("mde,mef->mdf", poly_term, iterate, preferred_element_type=jnp.float32)
        iterate = (coef_a * iterate.astype(jnp.float32) + mixed).astype(jnp.bfloat16)
    return iterate


def local(keys_a, values_a, queries_b, grad_out, state_start, state_next):
    tokens = keys_a.shape[1]
    block_shape = (tokens, H, D)
    key_rows = keys_a.reshape(block_shape)
    value_rows = values_a.reshape(block_shape)
    query_rows = queries_b.reshape(block_shape)
    out_rows = grad_out.reshape(block_shape)
    clip_next = state_next[0]
    ctx_count = lax.axis_size("ctx")
    per_dev = (H + ctx_count - 1) // ctx_count
    head_pad = per_dev * ctx_count - H
    token_pad = ((0, 0), (0, head_pad), (0, 0))
    state_pad = ((0, 0), (0, head_pad), (0, 0), (0, 0))
    padded = [jnp.pad(rows, token_pad) for rows in (key_rows, value_rows, query_rows, out_rows)]
    key_all, value_all, query_all, out_all = sent_together(
        (padded[0], padded[1], padded[2], padded[3]), "ctx", 1, 0, 2
    )
    start_pad = jnp.pad(state_start.astype(jnp.bfloat16), state_pad)
    next_pad = jnp.pad(clip_next.astype(jnp.bfloat16), state_pad)
    start_own, next_own = sent_together((start_pad, next_pad), "ctx", 1, 2, 0)
    blocks = (ctx_count, tokens, per_dev, D)
    key_blocks = key_all.reshape(blocks)
    value_blocks = value_all.reshape(blocks)
    query_blocks = query_all.reshape(blocks)
    out_blocks = out_all.reshape(blocks)
    parts_g = jax.vmap(field_grad, in_axes=(None, 0, 0))(start_own, key_blocks, value_blocks)
    total_g = jnp.sum(parts_g.astype(jnp.bfloat16).astype(jnp.float32), axis=0)
    parts_s = jax.vmap(field_grad, in_axes=(None, 0, 0))(next_own, query_blocks, out_blocks)
    total_s = jnp.sum(parts_s.astype(jnp.bfloat16).astype(jnp.float32), axis=0)
    own_slots = (3 * per_dev, D, F)
    d_update = (step_rate * total_s).astype(jnp.bfloat16).reshape(own_slots)
    unused, pullback = jax.vjp(newton, total_g.reshape(own_slots))
    d_field = pullback(d_update)[0].reshape(total_g.shape)

    def backward(key_block, value_block):
        unused_out, pull_block = jax.vjp(field_grad, start_own, key_block, value_block)
        return pull_block(d_field)

    d_start, d_keys, d_values = jax.vmap(backward)(key_blocks, value_blocks)
    summed = (parts_s + d_start.astype(jnp.float32)).astype(jnp.bfloat16).astype(jnp.float32)
    clip_heads = jnp.sum(summed, axis=0)
    back_shape = (ctx_count * tokens, per_dev, D)
    keys_back, values_back = sent_together(
        (d_keys.reshape(back_shape), d_values.reshape(back_shape)), "ctx", 0, 1, 2
    )
    rows_back = lax.all_to_all(
        clip_heads.astype(jnp.bfloat16), "ctx", split_axis=2, concat_axis=1, tiled=True
    ).astype(clip_heads.dtype)
    state_shard = rows_back[:, :H]
    d_keys_out = keys_back[:, :H].reshape(keys_a.shape)
    d_values_out = values_back[:, :H].reshape(values_a.shape)
    state_total = gathered_total(state_shard.astype(jnp.bfloat16), "dp").astype(jnp.float32)
    grad_state = state_total / lax.axis_size("dp")
    return (d_keys_out, d_values_out, grad_state)


def solution(mesh):
    placed = (
        P("dp", "ctx", None),
        P("dp", "ctx", None),
        P("dp", "ctx", None),
        P("dp", "ctx", None),
        P(None, None, "ctx", None),
        P("dp", None, None, "ctx", None),
    )
    return jax.shard_map(
        local,
        mesh=mesh,
        in_specs=placed,
        out_specs=(P("dp", "ctx", None), P("dp", "ctx", None), P(None, None, "ctx", None)),
        check_vma=False,
    )
```

profile of v0, /device:TPU:1, one launch (start us, length us, event | category | flops | bytes accessed | tf_op | source)
XLA Modules:
  0.0 310.5 jit_solution(6326290070212453705)
XLA Ops:
  7.2 1.1 copy.436
  8.3 1.8 fusion.112
  10.1 11.8 %all-to-all-start.1 = ((bf16[6,32,8,128]{3,2,0,1:T(8,128)(2,1)}), bf16[6,32,8,128]{3,2,0,1:T(8,128)(2,1)S(1)}, u32[]{:S(2)}, u32[]{:S(2)}) async-start(bf16[6,32,8,128]{3,2,0,1:T(8,128)(2,1)} %fusion.112), calls=%async_computation.1 | async-start | bytes 786432 | tf_op jit(solution)/shard_map/all_to_all | solution.py:21
  22.9 1.4 copy.212
  24.3 11.9 %fusion.8 = bf16[128,32,512]{0,2,1:T(8,128)(2,1)} fusion(bf16[128,20,128]{0,2,1:T(8,128)(2,1)S(1)} %bitcast.428, bf16[128,20,128]{0,2,1:T(8,128)(2,1)S(1)} %bitcast.427, bf16[128,20,128]{0,2,1:T(8,128)(2,1)S(1)} %bitcast.426, bf16[128,20,128]{0,2,1:T(8,128)(2,1)S(1)} %bitcast.425), kind=kLoop, calls=%fused_computation.19 | loop fusion | flops 41943040 | bytes 6815744 | tf_op jit(solution)/shard_map/concatenate | solution.py:20
  36.4 7.1 %all-to-all-start = ((bf16[128,32,512]{0,2,1:T(8,128)(2,1)}), bf16[128,32,512]{0,2,1:T(8,128)(2,1)}, u32[]{:S(2)}, u32[]{:S(2)}) async-start(bf16[128,32,512]{0,2,1:T(8,128)(2,1)} %fusion.8), calls=%async_computation | async-start | bytes 8388608 | tf_op jit(solution)/shard_map/all_to_all | solution.py:21
  44.3 92.7 %all-to-all-done = bf16[128,32,512]{0,2,1:T(8,128)(2,1)} async-done(((bf16[128,32,512]{0,2,1:T(8,128)(2,1)}), bf16[128,32,512]{0,2,1:T(8,128)(2,1)}, u32[]{:S(2)}, u32[]{:S(2)}) %all-to-all-start) | async-done | bytes 4194336 | tf_op jit(solution)/shard_map/all_to_all | solution.py:21
  137.0 6.6 %copy.213 = bf16[16,128,2,512]{3,1,0,2:T(8,128)(2,1)} copy(bf16[16,128,2,512]{1,3,2,0:T(8,128)(2,1)} %bitcast.5) | data formatting | bytes 8388608 | tf_op jit(solution)/shard_map/all_to_all | solution.py:21
  143.6 3.5 %fusion.158 = (bf16[2048,2,128]{2,0,1:T(8,128)(2,1)}, bf16[2048,2,128]{2,0,1:T(8,128)(2,1)S(1)}, bf16[2048,2,128]{2,0,1:T(8,128)(2,1)S(1)}, bf16[2048,2,128]{2,0,1:T(8,128)(2,1)S(1)}) fusion(bf16[2048,2,512]{2,0,1:T(8,128)(2,1)} %bitcast.405), kind=kLoop, calls=%fused_computation.237 | loop fusion | bytes 8388608 | tf_op jit(solution)/shard_map/split | solution.py:22
  148.1 2.9 fusion.30
  157.4 1.5 fusion.39
  159.9 0.9 convolution_bitcast_fusion.1
  162.5 1.0 copy-done.4
  164.6 0.9 convolution_convert_fusion.16
  166.4 1.4 fusion.85
  169.0 10.9 %convolution_convert_fusion.9 = bf16[6,128,128]{2,1,0:T(8,128)(2,1)} fusion(bf16[6,128,128]{2,1,0:T(8,128)(2,1)S(1)} %fusion.93, bf16[6,128,128]{2,1,0:T(8,128)(2,1)S(1)} %copy-done.7), kind=kOutput, calls=%fused_computation.123 | convolution fusion | flops 25264128 | bytes 589824 | tf_op jit(solution)/shard_map/transpose(jvp(mdf,mef->mde))/dot_general | solution.py:53
  180.0 1.5 fusion.114
  183.9 3.1 %fusion.14 = (bf16[16,2,128,128]{3,2,0,1:T(8,128)(2,1)S(1)}, bf16[16,2,128,128]{3,2,0,1:T(8,128)(2,1)S(1)}, bf16[16,2,128,128]{3,2,0,1:T(8,128)(2,1)S(1)}) fusion(f32[2,128,16,128]{3,1,2,0:T(8,128)S(1)} %copy-done.39, f32[2,128,16,128]{3,1,2,0:T(8,128)S(1)} %copy-done.20, bf16[2,128,16,128]{3,1,2,0:T(8,128)(2,1)S(1)} %convolution_convert_fusion.4, ...), kind=kOutput, calls=%fused_computation.28 | convolution fusion | flops 154664960 | bytes 12648448 | tf_op jit(solution)/shard_map/vmap(transpose(jvp(thd,thf->hdf)))/dot_general | solution.py:43
  191.1 1.0 fusion.10
  192.3 15.6 %all_to_all.60 = bf16[3,2,128,128]{3,1,0,2:T(2,128)(2,1)S(1)} all-to-all(bf16[3,2,128,128]{3,1,0,2:T(2,128)(2,1)S(1)} %copy.265), channel_id=1, replica_groups=mesh['dp'=32,'ctx'=16] {'ctx'}, dimensions={2} | all-to-all | bytes 393216 | tf_op jit(solution)/shard_map/all_to_all | solution.py:110
  208.7 2.4 copy.247
  211.1 1.4 copy.248
  213.1 1.7 fusion.161
  217.5 8.7 %copy.256 = bf16[2048,2,128]{2,1,0:T(2,128)(2,1)S(1)} copy(bf16[2048,2,128]{2,0,1:T(8,128)(2,1)S(1)} %bitcast.420) | data formatting | bytes 2097152 | tf_op jit(solution)/shard_map/reshape | solution.py:108
  227.9 8.9 %copy.257 = bf16[2048,2,128]{2,1,0:T(2,128)(2,1)S(1)} copy(bf16[2048,2,128]{2,0,1:T(8,128)(2,1)S(1)} %bitcast.421) | data formatting | bytes 2097152 | tf_op jit(solution)/shard_map/reshape | solution.py:108
  236.8 2.3 pad_maximum_fusion
  239.1 53.7 %all_to_all.61 = bf16[2048,2,256]{2,1,0:T(2,128)(2,1)S(1)} all-to-all(bf16[2048,2,256]{2,1,0:T(2,128)(2,1)S(1)} %pad_maximum_fusion), channel_id=1, replica_groups=mesh['dp'=32,'ctx'=16] {'ctx'}, dimensions={0} | all-to-all | bytes 4194304 | tf_op jit(solution)/shard_map/all_to_all | solution.py:21
  292.8 3.7 %copy.258 = bf16[16,128,2,256]{1,3,2,0:T(8,128)(2,1)} copy(bf16[16,128,2,256]{3,2,1,0:T(2,128)(2,1)S(1)} %bitcast.415) | data formatting | bytes 4194304 | tf_op jit(solution)/shard_map/all_to_all | solution.py:21
  296.5 1.4 fusion.159
  297.8 1.1 copy.268
  298.9 1.1 copy.269
  300.0 2.7 convert_reduce_fusion
  (136 shorter events, 27.9 us)
Async XLA Ops:
  7.2 14.7 %copy-start.27 = (bf16[1,128,2560]{2,1,0:T(8,128)(2,1)S(1)}, bf16[1,128,2560]{2,1,0:T(8,128)(2,1)}, u32[]{:S(2)}) copy-start(bf16[1,128,2560]{2,1,0:T(8,128)(2,1)} %param.6) | copy-start | bytes 1966084
  7.2 15.0 %copy-start.28 = (bf16[1,128,2560]{2,1,0:T(8,128)(2,1)S(1)}, bf16[1,128,2560]{2,1,0:T(8,128)(2,1)}, u32[]{:S(2)}) copy-start(bf16[1,128,2560]{2,1,0:T(8,128)(2,1)} %param.7) | copy-start | bytes 1966084
  8.3 14.3 %copy-start.29 = (bf16[1,128,2560]{2,1,0:T(8,128)(2,1)S(1)}, bf16[1,128,2560]{2,1,0:T(8,128)(2,1)}, u32[]{:S(2)}) copy-start(bf16[1,128,2560]{2,1,0:T(8,128)(2,1)} %param.8) | copy-start | bytes 1966084
  10.1 26.3 %all-to-all-start.1 = ((bf16[6,32,8,128]{3,2,0,1:T(8,128)(2,1)}), bf16[6,32,8,128]{3,2,0,1:T(8,128)(2,1)S(1)}, u32[]{:S(2)}, u32[]{:S(2)}) async-start(bf16[6,32,8,128]{3,2,0,1:T(8,128)(2,1)} %fusion.112), calls=%async_computation.1 | async-start | bytes 786432 | tf_op jit(solution)/shard_map/all_to_all | solution.py:21
  36.4 100.6 %all-to-all-start = ((bf16[128,32,512]{0,2,1:T(8,128)(2,1)}), bf16[128,32,512]{0,2,1:T(8,128)(2,1)}, u32[]{:S(2)}, u32[]{:S(2)}) async-start(bf16[128,32,512]{0,2,1:T(8,128)(2,1)} %fusion.8), calls=%async_computation | async-start | bytes 8388608 | tf_op jit(solution)/shard_map/all_to_all | solution.py:21
  43.5 256.6 %all-gather.3.cloned.1.call-start = ((), (), s32[]{:S(2)}) async-start(), calls=%async_computation.4 | async-start | bytes 4055040 | tf_op jit(solution)/shard_map/all_gather | solution.py:26
  44.2 102.9 %copy-start.32 = (bf16[1,2,16,8,128]{4,3,1,2,0:T(8,128)(2,1)}, bf16[1,2,16,8,128]{4,3,1,2,0:T(8,128)(2,1)S(1)}, u32[]{:S(2)}) copy-start(bf16[1,2,16,8,128]{4,3,1,2,0:T(8,128)(2,1)S(1)} %get-tuple-element.32) | copy-start | bytes 196612
  44.2 103.4 %copy-start.30 = (bf16[1,2,16,8,128]{4,3,1,2,0:T(8,128)(2,1)}, bf16[1,2,16,8,128]{4,3,1,2,0:T(8,128)(2,1)S(1)}, u32[]{:S(2)}) copy-start(bf16[1,2,16,8,128]{4,3,1,2,0:T(8,128)(2,1)S(1)} %get-tuple-element.33) | copy-start | bytes 196612
  44.3 103.9 %copy-start.34 = (bf16[1,2,16,8,128]{4,3,1,2,0:T(8,128)(2,1)}, bf16[1,2,16,8,128]{4,3,1,2,0:T(8,128)(2,1)S(1)}, u32[]{:S(2)}) copy-start(bf16[1,2,16,8,128]{4,3,1,2,0:T(8,128)(2,1)S(1)} %get-tuple-element.31) | copy-start | bytes 196612
  147.6 3.5 %copy-start.19 = (f32[2,128,16,128]{3,1,2,0:T(8,128)}, f32[2,128,16,128]{3,1,2,0:T(8,128)S(1)}, u32[]{:S(2)}) copy-start(f32[2,128,16,128]{3,1,2,0:T(8,128)S(1)} %fusion.132) | copy-start | bytes 6291460
  148.1 3.0 copy-start.21
  151.1 1.9 copy-start.15
  151.1 1.9 copy-start.11
  154.6 1.5 copy-start.37
  155.0 1.6 copy-start.8
  155.0 1.6 copy-start.36
  159.9 1.8 copy-start
  160.8 1.4 copy-start.2
  162.1 1.4 copy-start.4
  164.0 3.9 %copy-start.7 = (bf16[6,128,128]{2,1,0:T(8,128)(2,1)S(1)}, bf16[6,128,128]{2,1,0:T(8,128)(2,1)}, u32[]{:S(2)}) copy-start(bf16[6,128,128]{2,1,0:T(8,128)(2,1)} %copy-done.6) | copy-start | bytes 589828
  164.3 3.9 %copy-start.24 = (bf16[6,128,128]{2,1,0:T(8,128)(2,1)S(1)}, bf16[6,128,128]{2,1,0:T(8,128)(2,1)}, u32[]{:S(2)}) copy-start(bf16[6,128,128]{2,1,0:T(8,128)(2,1)} %copy-done.23) | copy-start | bytes 589828
  167.9 12.1 %copy-start.26 = (bf16[6,128,128]{2,1,0:T(8,128)(2,1)S(1)}, bf16[6,128,128]{2,1,0:T(8,128)(2,1)}, u32[]{:S(2)}) copy-start(bf16[6,128,128]{2,1,0:T(8,128)(2,1)} %copy-done.25) | copy-start | bytes 589828
  180.0 2.7 copy-start.39
  181.6 1.6 copy-start.20
  181.6 2.2 copy-start.22
  187.0 1.9 copy-start.17
  188.0 1.8 copy-start.3
  188.0 2.2 copy-start.5
  188.9 2.2 copy-start.1
  192.1 19.0 %copy-start.14 = (bf16[16,128,2,128]{1,3,0,2:T(8,128)(2,1)S(1)}, bf16[16,128,2,128]{1,3,0,2:T(8,128)(2,1)}, u32[]{:S(2)}) copy-start(bf16[16,128,2,128]{1,3,0,2:T(8,128)(2,1)} %copy-done.13) | copy-start | bytes 3145732
  208.7 3.7 %copy-start.12 = (bf16[16,128,2,128]{1,3,0,2:T(8,128)(2,1)S(1)}, bf16[16,128,2,128]{1,3,0,2:T(8,128)(2,1)}, u32[]{:S(2)}) copy-start(bf16[16,128,2,128]{1,3,0,2:T(8,128)(2,1)} %copy-done.11) | copy-start | bytes 3145732
  213.1 1.8 copy-start.16
  (11 other events, 10.6 us)
Sparse Core Ops, SparseCore 0:
  208.8 79.4 all-gather.2
where the time goes:
time: 316 us; the launch traced here: 311 us
  waiting for transfers between devices  92.9 us (29%)
  blocking collectives  69.3 us (22%)
  local copies, waits for them, and re-layouts  51.6 us (16%)
  matrix products  41.1 us (13%)
  other arithmetic  21.8 us (7%)
  starting transfers between devices  18.9 us (6%)
  between operations  14.9 us (5%)
    all_to_all x2, waiting for transfers between devices, sent_together(): lax.all_to_all(both, axis, split_axis=split_dim, concat_axis=concat_dim,...  92.9 us
    all_to_all x1, blocking collectives, sent_together(): lax.all_to_all(both, axis, split_axis=split_dim, concat_axis=concat_dim,...  53.7 us
    all_to_all x2, starting transfers between devices, sent_together(): lax.all_to_all(both, axis, split_axis=split_dim, concat_axis=concat_dim,...  18.9 us
    concatenate x3, other arithmetic, sent_together(): both = jnp.concatenate(arrays, axis=along)  16 us
    all_to_all x1, blocking collectives, local(): lax.all_to_all(clip_heads.astype(jnp.bfloat16), 'ctx', split_axis=2, conc...  15.6 us
    dot_general x6, matrix products, newton(): jnp.einsum('mdf,mef->mde', iterate, iterate, preferred_element_type=jnp.f...  13.5 us
    unnamed x87, local copies, waits for them, and re-layouts  12.6 us
    all_to_all x3, local copies, waits for them, and re-layouts, sent_together(): lax.all_to_all(both, axis, split_axis=split_dim, concat_axis=concat_dim,...  10.3 us
  transfers between devices with their start and end apart: 3, of which 2 were waited for; matrix products, arithmetic and copies ran while one was open for 16% of the time, Pallas kernels for 0%

commit v1 on v0

v1 whole, which is shorter than its diff:
```python
import functools

import jax
import jax.numpy as jnp
from jax import lax
from jax.experimental import pallas as pl
from jax.experimental.pallas import tpu as pltpu
from jax.sharding import PartitionSpec as P

D = 128
H = 20
F = 128
HH = H // 2
RATE = 4.0
CA = 3.4445
CB = -4.775
CC = 2.0315
MESH = pl.DeviceIdType.MESH
F32 = jnp.float32
BF16 = jnp.bfloat16


def mm(a, b):
    return jnp.dot(a, b, preferred_element_type=F32)


def mm_tn(a, b):
    return lax.dot_general(a, b, (((0,), (0,)), ((), ())), preferred_element_type=F32)


def mm_nt(a, b):
    return lax.dot_general(a, b, (((1,), (1,)), ((), ())), preferred_element_type=F32)


def newton_forward(mats):
    norms, units, xs, grams, polys = [], [], [], [], []
    for g in mats:
        total = jnp.sum(jnp.sum(g * g, axis=1, keepdims=True), axis=0, keepdims=True)
        n = jnp.sqrt(total + 1e-06)
        u = g / n
        norms.append(n)
        units.append(u)
    x = [u.astype(BF16) for u in units]
    for step in range(2):
        a = [mm_nt(v, v).astype(BF16) for v in x]
        sq = [mm(v, v) for v in a]
        p = [(CB * v.astype(F32) + CC * w).astype(BF16) for v, w in zip(a, sq)]
        xs.append(x)
        grams.append(a)
        polys.append(p)
        if step == 0:
            mixed = [mm(v, w) for v, w in zip(p, x)]
            x = [(CA * v.astype(F32) + w).astype(BF16) for v, w in zip(x, mixed)]
    return norms, units, xs, grams, polys


def newton_backward(saved, cts):
    norms, units, xs, grams, polys = saved
    ct = cts
    for step in (1, 0):
        x, a, p = xs[step], grams[step], polys[step]
        ct_z = [mm_nt(v, w).astype(BF16) for v, w in zip(ct, x)]
        direct = [CA * v.astype(F32) + mm(w, v) for v, w in zip(ct, p)]
        ct_a = [
            (CB * v.astype(F32) + CC * (mm(v, w) + mm(w, v))).astype(BF16)
            for v, w in zip(ct_z, a)
        ]
        ct = [
            (d + mm(v, w) + mm_tn(v, w)).astype(BF16) for d, v, w in zip(direct, ct_a, x)
        ]
    out = []
    for n, u, v in zip(norms, units, ct):
        v = v.astype(F32)
        dot = jnp.sum(jnp.sum(v * u, axis=1, keepdims=True), axis=0, keepdims=True)
        out.append((v - u * dot) / n)
    return out


def main_kernel(
    nz,
    keys, values, queries, gout, start, nxt,
    dk_out, dv_out, part_out,
    xk, xv, xq, xo, stage, ws, wn, gbuf, sbuf, psum,
    rs_send, rs_recv, field, act, rnd, dk, dv, tot, gr_send, gr_recv,
    in_sem, x_ssem, x_rsem, ag_ssem, ag_rsem, rs_ssem, rs_rsem,
    f_ssem, f_rsem, gr_ssem, gr_rsem, o_sem, o_ssem, o_rsem,
):
    ctx = lax.axis_index("ctx")
    z = lax.div(ctx, 2)
    c = lax.rem(ctx, 2)
    other = 1 - c

    def chip(offset):
        return lax.rem(z + offset + 2 * nz, nz)

    right = 2 * chip(1) + c
    left = 2 * chip(-1) + c
    partner = 2 * z + other
    half = HH * D
    dirs = ((right, 1), (left, -1))
    far = nz // 2

    barrier = pltpu.get_barrier_semaphore()
    for peer in (right, left, partner):
        pl.semaphore_signal(barrier, inc=1, device_id={"ctx": peer}, device_id_type=MESH)
    pl.semaphore_wait(barrier, 3)

    def remote(src, dst, ssem, rsem, peer):
        return pltpu.make_async_remote_copy(
            src_ref=src, dst_ref=dst, send_sem=ssem, recv_sem=rsem,
            device_id={"ctx": peer}, device_id_type=MESH,
        )

    own_heads = pl.ds(c * HH, HH)
    other_heads = pl.ds(other * HH, HH)
    own_cols = pl.ds(pl.multiple_of(c * half, 128), half)
    other_cols = pl.ds(pl.multiple_of(other * half, 128), half)
    tokens = keys.shape[0]

    sends = []
    locals_in, remotes_in = [], []
    for k, st in enumerate((start, nxt)):
        cp = remote(st.at[:, other_heads], stage.at[k, c], x_ssem.at[k], x_rsem.at[k], partner)
        cp.start()
        remotes_in.append(cp)
        lc = pltpu.make_async_copy(st.at[:, own_heads], stage.at[k, 2], in_sem.at[k])
        lc.start()
        locals_in.append(lc)
    for k, (src, dst) in enumerate(((keys, xk), (values, xv), (queries, xq), (gout, xo))):
        cp = remote(
            src.at[:, other_cols], dst.at[tokens : 2 * tokens],
            x_ssem.at[2 + k], x_rsem.at[2 + k], partner,
        )
        cp.start()
        remotes_in.append(cp)
        lc = pltpu.make_async_copy(src.at[:, own_cols], dst.at[0:tokens], in_sem.at[2 + k])
        lc.start()
        locals_in.append(lc)
    sends.extend(remotes_in)

    def rows_of(offset):
        return pl.ds(pl.multiple_of(16 * chip(offset), 16), 16)

    weights = (ws, wn)
    for k in range(2):
        locals_in[k].wait()
        remotes_in[k].wait_recv()
        mine = stage[k, 2]
        theirs = stage[k, other]
        for comp in range(3):
            top = jnp.where(c == 0, mine[comp], theirs[comp])
            low = jnp.where(c == 0, theirs[comp], mine[comp])
            weights[k][:, rows_of(0), comp * F : (comp + 1) * F] = jnp.concatenate(
                [top, low], axis=1
            ).astype(BF16)

    def ag_copy(k, dr, step):
        peer, sign = dirs[dr]
        heads = pl.ds(0, HH)
        if step == far:
            heads = pl.ds(0, HH // 2) if dr == 0 else pl.ds(HH // 2, HH - HH // 2)
        piece = weights[k].at[heads, rows_of(-sign * (step - 1)), :]
        return remote(piece, piece, ag_ssem.at[k, dr, step - 1], ag_rsem.at[k, dr, step - 1], peer)

    ag = {}
    for step in range(1, far + 1):
        for k in range(2):
            for dr in range(2):
                if step > 1:
                    ag[k, dr, step - 1].wait_recv()
                cp = ag_copy(k, dr, step)
                cp.start()
                ag[k, dr, step] = cp
                sends.append(cp)
    for k in range(4):
        locals_in[2 + k].wait()
        remotes_in[2 + k].wait_recv()

    def phi(h, xs, ys, w):
        cols = pl.ds(pl.multiple_of(h * D, 128), D)
        x, y = xs[:, cols], ys[:, cols]
        wh = w[h]
        gu = mm(x, wh[:, : 2 * F])
        proj = mm(y, wh[:, 2 * F :])
        gate, up = gu[:, :F], gu[:, F:]
        s = jax.nn.sigmoid(gate)
        swish = gate * s
        hidden = (swish * up).astype(BF16)
        d_gate = (proj * up * s * (1.0 + gate * (1.0 - s))).astype(BF16)
        d_up = (proj * swish).astype(BF16)
        gab = mm_tn(x, jnp.concatenate([d_gate, d_up], axis=1))
        gc = mm_tn(y, hidden)
        return gate, up, proj, hidden, d_gate, d_up, gab, gc

    def phi_a(h, carry):
        gate, up, proj, hidden, d_gate, d_up, gab, gc = phi(h, xk, xv, ws)
        act[h, 0] = gate
        act[h, 1] = up
        act[h, 2] = proj
        rnd[h, 0] = d_gate
        rnd[h, 1] = d_up
        rnd[h, 2] = hidden
        gbuf[3 * h] = gab[:, :F].astype(BF16)
        gbuf[3 * h + 1] = gab[:, F:].astype(BF16)
        gbuf[3 * h + 2] = gc.astype(BF16)
        return carry

    def phi_b(h, carry):
        _, _, _, _, _, _, gab, gc = phi(h, xq, xo, wn)
        psum[h, :, : 2 * F] = gab
        psum[h, :, 2 * F :] = gc
        sbuf[3 * h] = gab[:, :F].astype(BF16)
        sbuf[3 * h + 1] = gab[:, F:].astype(BF16)
        sbuf[3 * h + 2] = gc.astype(BF16)
        return carry

    for pad in (3 * HH, 3 * HH + 1):
        gbuf[pad] = jnp.zeros((D, F), BF16)
        sbuf[pad] = jnp.zeros((D, F), BF16)

    bufs = (gbuf, sbuf)
    rs = {}

    def rs_step(k, step):
        for dr, (peer, sign) in enumerate(dirs):
            base = pl.multiple_of(4 * chip(sign * (far + 1 - step)), 4)
            lo, cnt = (0, 4)
            if step == 1:
                lo, cnt = (0, 2) if dr == 0 else (2, 2)
            value = bufs[k][pl.ds(base + lo, cnt)]
            if step > 1:
                rs[k, dr, step - 1].wait_recv()
                if step == 2:
                    plo = 0 if dr == 0 else 2
                    for j in range(4):
                        v = bufs[k][base + j]
                        if plo <= j < plo + 2:
                            v = (v.astype(F32) + rs_recv[k, dr, 0, j].astype(F32)).astype(BF16)
                        rs_send[k, dr, 1, j] = v
                else:
                    total = value.astype(F32) + rs_recv[k, dr, step - 2].astype(F32)
                    rs_send[k, dr, step - 1] = total.astype(BF16)
                src = rs_send.at[k, dr, step - 1]
            else:
                src = bufs[k].at[pl.ds(base + lo, cnt)]
            dst = rs_recv.at[k, dr, step - 1, pl.ds(lo, cnt)]
            cp = remote(src, dst, rs_ssem.at[k, dr, step - 1], rs_rsem.at[k, dr, step - 1], peer)
            cp.start()
            rs[k, dr, step] = cp
            sends.append(cp)

    def rs_total(k):
        out = []
        for dr in range(2):
            rs[k, dr, far].wait_recv()
        base = pl.multiple_of(4 * z, 4)
        for j in range(4):
            v = bufs[k][base + j].astype(F32)
            v = v + rs_recv[k, 0, far - 1, j].astype(F32) + rs_recv[k, 1, far - 1, j].astype(F32)
            out.append(v)
        return out

    ag[0, 0, far].wait_recv()
    ag[0, 1, far].wait_recv()
    lax.fori_loop(0, HH, phi_a, 0)
    rs_step(0, 1)
    ag[1, 0, far].wait_recv()
    ag[1, 1, far].wait_recv()
    cuts = [HH * i // far for i in range(far + 1)]
    for i in range(far):
        lax.fori_loop(cuts[i], cuts[i + 1], phi_b, 0)
        if i + 2 <= far:
            rs_step(0, i + 2)
    rs_step(1, 1)
    saved = newton_forward(rs_total(0))
    for step in range(2, far + 1):
        rs_step(1, step)
    cts = [(RATE * v).astype(BF16) for v in rs_total(1)]
    fields = newton_backward(saved, cts)
    for j in range(4):
        field[pl.multiple_of(4 * z, 4) + j] = fields[j].astype(BF16)

    fd = {}
    for step in range(1, far + 1):
        for dr, (peer, sign) in enumerate(dirs):
            if step > 1:
                fd[dr, step - 1].wait_recv()
            base = pl.multiple_of(4 * chip(-sign * (step - 1)), 4)
            lo, cnt = (0, 4)
            if step == far:
                lo, cnt = (0, 2) if dr == 0 else (2, 2)
            piece = field.at[pl.ds(base + lo, cnt)]
            cp = remote(piece, piece, f_ssem.at[dr, step - 1], f_rsem.at[dr, step - 1], peer)
            cp.start()
            fd[dr, step] = cp
            sends.append(cp)
    fd[0, far].wait_recv()
    fd[1, far].wait_recv()

    def back(h, carry):
        cols = pl.ds(pl.multiple_of(h * D, 128), D)
        x, y = xk[:, cols], xv[:, cols]
        gate, up, proj = act[h, 0], act[h, 1], act[h, 2]
        d_gate, d_up, hidden = rnd[h, 0], rnd[h, 1], rnd[h, 2]
        da, db, dc = field[3 * h], field[3 * h + 1], field[3 * h + 2]
        dab = jnp.concatenate([da, db], axis=1)
        ct_gu = mm(x, dab).astype(BF16).astype(F32)
        ct_dg, ct_du = ct_gu[:, :F], ct_gu[:, F:]
        ct_h = mm(y, dc).astype(BF16).astype(F32)
        s = jax.nn.sigmoid(gate)
        swish = gate * s
        sd = s * (1.0 - s)
        q = s + gate * sd
        qd = sd * (2.0 + gate * (1.0 - 2.0 * s))
        ct_w = ct_h * up + ct_du * proj
        cq = ct_dg * q
        ct_up = (ct_h * swish + cq * proj).astype(BF16)
        ct_p = (ct_du * swish + cq * up).astype(BF16)
        ct_gate = (ct_w * q + ct_dg * (proj * up) * qd).astype(BF16)
        wh = ws[h]
        ct_ab = jnp.concatenate([ct_gate, ct_up], axis=1)
        d_ab = jnp.concatenate([d_gate, d_up], axis=1)
        dx = mm_nt(d_ab, dab) + mm_nt(ct_ab, wh[:, : 2 * F])
        dy = mm_nt(hidden, dc) + mm_nt(ct_p, wh[:, 2 * F :])
        dk[:, cols] = dx.astype(BF16)
        dv[:, cols] = dy.astype(BF16)
        tot[h, :, : 2 * F] = (psum[h, :, : 2 * F] + mm_tn(x, ct_ab)).astype(BF16)
        tot[h, :, 2 * F :] = (psum[h, :, 2 * F :] + mm_tn(y, ct_p)).astype(BF16)
        return carry

    lax.fori_loop(0, HH, back, 0)

    outs = []
    for k, (src, dst) in enumerate(((dk, dk_out), (dv, dv_out))):
        cp = remote(src.at[tokens : 2 * tokens], dst.at[:, own_cols], o_ssem.at[k], o_rsem.at[k], partner)
        lc = pltpu.make_async_copy(src.at[0:tokens], dst.at[:, own_cols], o_sem.at[k])
        outs.append((cp, lc))

    gr = {}
    for step in range(1, far + 1):
        for dr, (peer, sign) in enumerate(dirs):
            rows = rows_of(sign * (far + 1 - step))
            lo, cnt = 0, HH
            if step == 1:
                lo, cnt = (0, HH // 2) if dr == 0 else (HH // 2, HH - HH // 2)
                src = tot.at[pl.ds(lo, cnt), rows, :]
            else:
                gr[dr, step - 1].wait_recv()
                if step == 2:
                    a, b = (0, HH // 2) if dr == 0 else (HH // 2, HH)
                    own = tot[a:b, rows, :].astype(F32) + gr_recv[dr, 0, a:b].astype(F32)
                    gr_send[dr, 1, a:b] = own.astype(BF16)
                    a, b = (HH // 2, HH) if dr == 0 else (0, HH // 2)
                    gr_send[dr, 1, a:b] = tot[a:b, rows, :]
                else:
                    own = tot[:, rows, :].astype(F32) + gr_recv[dr, step - 2].astype(F32)
                    gr_send[dr, step - 1] = own.astype(BF16)
                src = gr_send.at[dr, step - 1]
            dst = gr_recv.at[dr, step - 1, pl.ds(lo, cnt)]
            cp = remote(src, dst, gr_ssem.at[dr, step - 1], gr_rsem.at[dr, step - 1], peer)
            cp.start()
            gr[dr, step] = cp
            sends.append(cp)
        if step == 1:
            for cp, lc in outs:
                cp.start()
                lc.start()
    gr[0, far].wait_recv()
    gr[1, far].wait_recv()
    own = tot[:, rows_of(0), :].astype(F32)
    own = own + gr_recv[0, far - 1].astype(F32) + gr_recv[1, far - 1].astype(F32)
    own = own.astype(BF16)
    for h in range(HH):
        for comp in range(3):
            part_out[3 * h + comp] = own[h, :, comp * F : (comp + 1) * F]
    part_out[3 * HH] = jnp.zeros((16, F), BF16)
    part_out[3 * HH + 1] = jnp.zeros((16, F), BF16)

    for cp in sends:
        cp.wait_send()
    for cp, lc in outs:
        cp.wait_send()
        cp.wait_recv()
        lc.wait()


def dp_kernel(n, part, out, land, fin, stage, s1, r1, s2, r2, o_sem, o_ssem, o_rsem):
    ctx = lax.axis_index("ctx")
    c = lax.rem(ctx, 2)
    other = 1 - c
    partner = ctx + 1 - 2 * c
    me = lax.axis_index("dp")
    barrier = pltpu.get_barrier_semaphore()

    def peer_of(k):
        return lax.rem(me + k, n)

    def greet(k, carry):
        pl.semaphore_signal(barrier, inc=1, device_id={"dp": peer_of(k)}, device_id_type=MESH)
        return carry

    lax.fori_loop(1, n, greet, 0)
    pl.semaphore_signal(barrier, inc=1, device_id={"ctx": partner}, device_id_type=MESH)
    pl.semaphore_wait(barrier, n)

    def scatter(k):
        j = peer_of(k)
        return pltpu.make_async_remote_copy(
            src_ref=part.at[j], dst_ref=land.at[k], send_sem=s1.at[k], recv_sem=r1.at[k],
            device_id={"dp": j}, device_id_type=MESH,
        )

    def spread(k):
        j = peer_of(k)
        return pltpu.make_async_remote_copy(
            src_ref=fin.at[me], dst_ref=fin.at[me], send_sem=s2.at[k], recv_sem=r2.at[k],
            device_id={"dp": j}, device_id_type=MESH,
        )

    def start1(k, carry):
        scatter(k).start()
        return carry

    def wait1(k, total):
        scatter(k).wait_recv()
        return total + land[k].astype(F32)

    lax.fori_loop(1, n, start1, 0)
    total = lax.fori_loop(1, n, wait1, part[me].astype(F32))
    fin[me] = (total / n).astype(BF16)

    def start2(k, carry):
        spread(k).start()
        return carry

    def wait2(k, carry):
        spread(k).wait_recv()
        return carry

    lax.fori_loop(1, n, start2, 0)
    lax.fori_loop(1, n, wait2, 0)
    for h in range(HH):
        for comp in range(3):
            rows = fin[3 * h + comp].astype(F32)
            stage[0, comp, h] = rows[:8]
            stage[1, comp, h] = rows[8:]
    heads = pl.ds(c * HH, HH)
    cp = pltpu.make_async_remote_copy(
        src_ref=stage.at[other], dst_ref=out.at[:, heads], send_sem=o_ssem, recv_sem=o_rsem,
        device_id={"ctx": partner}, device_id_type=MESH,
    )
    lc = pltpu.make_async_copy(stage.at[c], out.at[:, heads], o_sem)
    cp.start()
    lc.start()

    def wait_sent(k, carry):
        scatter(k).wait_send()
        spread(k).wait_send()
        return carry

    lax.fori_loop(1, n, wait_sent, 0)
    cp.wait()
    lc.wait()


def ring_call(n_ctx, keys_a, values_a, queries_b, grad_out, state_start, state_next):
    tokens = keys_a.shape[1]
    nz = n_ctx // 2
    far = nz // 2
    anyspace = pl.BlockSpec(memory_space=pl.ANY)
    vm = pl.BlockSpec(memory_space=pltpu.VMEM)
    flat = (tokens, H * D)
    dma = pltpu.SemaphoreType.DMA
    rows2 = 2 * tokens
    half = HH * D
    dk, dv, part = pl.pallas_call(
        functools.partial(main_kernel, nz),
        out_shape=(
            jax.ShapeDtypeStruct(flat, BF16),
            jax.ShapeDtypeStruct(flat, BF16),
            jax.ShapeDtypeStruct((32, 16, F), BF16),
        ),
        in_specs=[anyspace] * 6,
        out_specs=(anyspace, anyspace, vm),
        scratch_shapes=[
            pltpu.VMEM((rows2, half), BF16),
            pltpu.VMEM((rows2, half), BF16),
            pltpu.VMEM((rows2, half), BF16),
            pltpu.VMEM((rows2, half), BF16),
            pltpu.VMEM((2, 3, 3, HH, 8, F), F32),
            pltpu.VMEM((HH, D, 3 * F), BF16),
            pltpu.VMEM((HH, D, 3 * F), BF16),
            pltpu.VMEM((32, D, F), BF16),
            pltpu.VMEM((32, D, F), BF16),
            pltpu.VMEM((HH, D, 3 * F), F32),
            pltpu.VMEM((2, 2, far, 4, D, F), BF16),
            pltpu.VMEM((2, 2, far, 4, D, F), BF16),
            pltpu.VMEM((32, D, F), BF16),
            pltpu.VMEM((HH, 3, rows2, F), F32),
            pltpu.VMEM((HH, 3, rows2, F), BF16),
            pltpu.VMEM((rows2, half), BF16),
            pltpu.VMEM((rows2, half), BF16),
            pltpu.VMEM((HH, D, 3 * F), BF16),
            pltpu.VMEM((2, far, HH, 16, 3 * F), BF16),
            pltpu.VMEM((2, far, HH, 16, 3 * F), BF16),
            dma((6,)),
            dma((6,)),
            dma((6,)),
            dma((2, 2, far)),
            dma((2, 2, far)),
            dma((2, 2, far)),
            dma((2, 2, far)),
            dma((2, far)),
            dma((2, far)),
            dma((2, far)),
            dma((2, far)),
            dma((2,)),
            dma((2,)),
            dma((2,)),
        ],
        compiler_params=pltpu.CompilerParams(
            collective_id=0, has_side_effects=True, vmem_limit_bytes=56 * 1024 * 1024
        ),
        name="ttt_ring",
    )(
        keys_a.reshape(flat),
        values_a.reshape(flat),
        queries_b.reshape(flat),
        grad_out.reshape(flat),
        state_start,
        state_next[0],
    )
    return dk, dv, part


def dp_call(n_dp, part):
    anyspace = pl.BlockSpec(memory_space=pl.ANY)
    vm = pl.BlockSpec(memory_space=pltpu.VMEM)
    dma = pltpu.SemaphoreType.DMA
    return pl.pallas_call(
        functools.partial(dp_kernel, n_dp),
        out_shape=jax.ShapeDtypeStruct((3, H, 8, F), F32),
        in_specs=[vm],
        out_specs=anyspace,
        scratch_shapes=[
            pltpu.VMEM((32, 16, F), BF16),
            pltpu.VMEM((32, 16, F), BF16),
            pltpu.VMEM((2, 3, HH, 8, F), F32),
            dma((n_dp,)),
            dma((n_dp,)),
            dma((n_dp,)),
            dma((n_dp,)),
            dma,
            dma,
            dma,
        ],
        compiler_params=pltpu.CompilerParams(collective_id=1, has_side_effects=True),
        name="dp_sum",
    )(part)


def local(n_dp, n_ctx, keys_a, *rest):
    dk, dv, part = ring_call(n_ctx, keys_a, *rest)
    grad_state = dp_call(n_dp, part)
    return dk.reshape(keys_a.shape), dv.reshape(keys_a.shape), grad_state


def solution(mesh):
    placed = (
        P("dp", "ctx", None),
        P("dp", "ctx", None),
        P("dp", "ctx", None),
        P("dp", "ctx", None),
        P(None, None, "ctx", None),
        P("dp", None, None, "ctx", None),
    )
    return jax.shard_map(
        functools.partial(local, mesh.shape["dp"], mesh.shape["ctx"]),
        mesh=mesh,
        in_specs=placed,
        out_specs=(P("dp", "ctx", None), P("dp", "ctx", None), P(None, None, "ctx", None)),
        check_vma=False,
    )
```

time: 316 us -> 142 us (0.45); the launches traced: 311 us -> 142 us
  Pallas kernels: 0 us -> 137 us
  waiting for transfers between devices: 92.9 us -> 0 us
  blocking collectives: 69.3 us -> 0 us
  local copies, waits for them, and re-layouts: 51.6 us -> 3.91 us
  matrix products: 41.1 us -> 0 us
  other arithmetic: 21.8 us -> 0 us
  starting transfers between devices: 18.9 us -> 0 us
  between operations: 14.9 us -> 0.66 us
    pallas_call x0 -> x2, Pallas kernels: none -> 137 us  [the longest x1 100 us: ring_call(): pl.pallas_call(functools.partial(main_kernel, nz), out_shape=(jax.ShapeDt...]
    all_to_all x2 -> x0, waiting for transfers between devices: 92.9 us -> none  [sent_together(): lax.all_to_all(both, axis, split_axis=split_dim, concat_axis=concat_dim,...]
    all_to_all x2 -> x0, blocking collectives: 69.3 us -> none  [the longest x1 53.7 us: sent_together(): lax.all_to_all(both, axis, split_axis=split_dim, concat_axis=concat_dim,...]
    dot_general x37 -> x0, matrix products: 38.5 us -> none  [the longest x6 13.5 us: newton(): jnp.einsum('mdf,mef->mde', iterate, iterate, preferred_element_type=jnp.f...]
    all_to_all x2 -> x0, starting transfers between devices: 18.9 us -> none  [sent_together(): lax.all_to_all(both, axis, split_axis=split_dim, concat_axis=concat_dim,...]
    reshape x2 -> x0, local copies, waits for them, and re-layouts: 17.5 us -> none  [the longest x1 8.86 us: local(): d_values.reshape(back_shape)]
    concatenate x3 -> x0, other arithmetic: 16 us -> none  [sent_together(): both = jnp.concatenate(arrays, axis=along)]
    all_to_all x4 -> x0, local copies, waits for them, and re-layouts: 10.4 us -> none  [the longest x3 10.3 us: sent_together(): lax.all_to_all(both, axis, split_axis=split_dim, concat_axis=concat_dim,...]
  transfers between devices with their start and end apart: 3 -> 0, of which waited for: 2 -> 0; matrix products, arithmetic and copies ran while one was open for 16% -> 0% of each run, Pallas kernels for 0% -> 0%
where the time goes in v1:
time: 142 us
  Pallas kernels  137 us (96%)
  local copies, waits for them, and re-layouts  3.91 us (3%)
    pallas_call x1, Pallas kernels, ring_call(): pl.pallas_call(functools.partial(main_kernel, nz), out_shape=(jax.ShapeDt...  100 us
    pallas_call x1, Pallas kernels, dp_call(): pl.pallas_call(functools.partial(dp_kernel, n_dp), out_shape=jax.ShapeDty...  37 us
    unnamed x7, local copies, waits for them, and re-layouts  3.91 us

profile of v1, /device:TPU:1, one launch (start us, length us, event | category | flops | bytes accessed | tf_op | source)
XLA Modules:
  0.0 142.0 jit_solution(11264683697054209884)
XLA Ops:
  0.6 100.4 %ttt_ring.1 = (bf16[128,2560]{1,0:T(8,128)(2,1)}, bf16[128,2560]{1,0:T(8,128)(2,1)}, bf16[32,16,128]{2,1,0:T(8,128)(2,1)}) custom-call(bf16[128,2560]{1,0:T(8,128)(2,1)} %bitcast.9, bf16[128,2560]{1,0:T(8,128)(2,1)} %bitcast.10, bf16[128,2560]{1,0:T(8,128)(2,1)} %bitcast.11, bf16[128,2560]{1,0:T(8,128)(2,1)} %bitcast.12, f32[3,20,8,128]{3,2,1,0:T(8,128)} %start.1, ...), custom_call_target="tpu_custom_call" | custom-call | tf_op jit(solution)/shard_map/ttt_ring/pallas_call | solution.py:476
  101.1 37.0 %dp_sum.1 = f32[3,20,8,128]{3,2,1,0:T(8,128)} custom-call(bf16[32,16,128]{2,1,0:T(8,128)(2,1)} %get-tuple-element.8.part), custom_call_target="tpu_custom_call" | custom-call | tf_op jit(solution)/shard_map/dp_sum/pallas_call | solution.py:540
  138.0 0.0 copy-start.1
  138.0 2.0 %copy.12 = bf16[1,128,2560]{2,1,0:T(8,128)(2,1)} copy(bf16[1,128,2560]{2,1,0:T(8,128)(2,1)} %bitcast.8) | data formatting | bytes 1310720
  140.1 0.0 copy-done.1
  140.1 0.0 copy-start
  140.1 0.8 copy.13
  140.9 0.3 copy-done
  141.3 0.7 copy.14
Async XLA Ops:
  138.0 2.0 %copy-start.1 = (bf16[128,2560]{1,0:T(8,128)(2,1)S(1)}, bf16[128,2560]{1,0:T(8,128)(2,1)}, u32[]{:S(2)}) copy-start(bf16[128,2560]{1,0:T(8,128)(2,1)} %get-tuple-element.7) | copy-start | bytes 1966084
  140.1 1.2 copy-start

commit v2 on v1

v2 whole, which is shorter than its diff:
```python
import functools

import jax
import jax.numpy as jnp
from jax import lax
from jax.experimental import pallas as pl
from jax.experimental.pallas import tpu as pltpu
from jax.sharding import PartitionSpec as P

D = 128
H = 20
F = 128
HH = H // 2
RATE = 4.0
CA = 3.4445
CB = -4.775
CC = 2.0315
MESH = pl.DeviceIdType.MESH
F32 = jnp.float32
BF16 = jnp.bfloat16


def mm(a, b):
    return jnp.dot(a, b, preferred_element_type=F32)


def mm_tn(a, b):
    return lax.dot_general(a, b, (((0,), (0,)), ((), ())), preferred_element_type=F32)


def mm_nt(a, b):
    return lax.dot_general(a, b, (((1,), (1,)), ((), ())), preferred_element_type=F32)


def newton_forward(mats):
    norms, units, xs, grams, polys = [], [], [], [], []
    for g in mats:
        total = jnp.sum(jnp.sum(g * g, axis=1, keepdims=True), axis=0, keepdims=True)
        n = jnp.sqrt(total + 1e-06)
        u = g / n
        norms.append(n)
        units.append(u)
    x = [u.astype(BF16) for u in units]
    for step in range(2):
        a = [mm_nt(v, v).astype(BF16) for v in x]
        sq = [mm(v, v) for v in a]
        p = [(CB * v.astype(F32) + CC * w).astype(BF16) for v, w in zip(a, sq)]
        xs.append(x)
        grams.append(a)
        polys.append(p)
        if step == 0:
            mixed = [mm(v, w) for v, w in zip(p, x)]
            x = [(CA * v.astype(F32) + w).astype(BF16) for v, w in zip(x, mixed)]
    return norms, units, xs, grams, polys


def newton_backward(saved, cts):
    norms, units, xs, grams, polys = saved
    ct = cts
    for step in (1, 0):
        x, a, p = xs[step], grams[step], polys[step]
        ct_z = [mm_nt(v, w).astype(BF16) for v, w in zip(ct, x)]
        direct = [CA * v.astype(F32) + mm(w, v) for v, w in zip(ct, p)]
        ct_a = [
            (CB * v.astype(F32) + CC * (mm(v, w) + mm(w, v))).astype(BF16)
            for v, w in zip(ct_z, a)
        ]
        ct = [
            (d + mm(v, w) + mm_tn(v, w)).astype(BF16) for d, v, w in zip(direct, ct_a, x)
        ]
    out = []
    for n, u, v in zip(norms, units, ct):
        v = v.astype(F32)
        dot = jnp.sum(jnp.sum(v * u, axis=1, keepdims=True), axis=0, keepdims=True)
        out.append((v - u * dot) / n)
    return out


NX = 4
PARTS = 4


def main_kernel(
    nz, ny, n_dp, merged,
    keys, values, queries, gout, start, nxt,
    *refs,
):
    if merged:
        dk_out, dv_out, grad_out = refs[:3]
        refs = refs[3:]
        dp_refs, refs = refs[:11], refs[11:]
        part = dp_refs[0]
    else:
        dk_out, dv_out, part = refs[:3]
        refs = refs[3:]
    (
        xk, xv, xq, xo, stage, ws, wn, gbuf, sbuf, psum,
        rs_send, rs_recv, field, act, rnd, dk, dv, tot, gr_send, gr_recv,
        in_sem, x_ssem, x_rsem, st_ssem, st_rsem, sx_ssem, sx_rsem, ag_ssem, ag_rsem,
        rs_ssem, rs_rsem, f_ssem, f_rsem, gr_ssem, gr_rsem, o_sem, o_ssem, o_rsem,
    ) = refs
    ctx = lax.axis_index("ctx")
    z = lax.div(ctx, 2)
    c = lax.rem(ctx, 2)
    other = 1 - c
    me = lax.axis_index("dp")
    xi = lax.div(me, ny)
    yi = lax.rem(me, ny)

    def chip(offset):
        return lax.rem(z + offset + 2 * nz, nz)

    def xpos(offset):
        return lax.rem(xi + offset + 2 * NX, NX)

    right = {"ctx": 2 * chip(1) + c}
    left = {"ctx": 2 * chip(-1) + c}
    partner = {"ctx": 2 * z + other}
    xright = {"dp": xpos(1) * ny + yi}
    xleft = {"dp": xpos(-1) * ny + yi}
    half = HH * D
    dirs = ((right, 1), (left, -1))
    xdirs = ((xright, 1), (xleft, -1))
    far = nz // 2

    own_heads = pl.ds(c * HH, HH)
    other_heads = pl.ds(other * HH, HH)
    own_cols = pl.ds(pl.multiple_of(c * half, 128), half)
    other_cols = pl.ds(pl.multiple_of(other * half, 128), half)
    tokens = keys.shape[0]

    locals_in = []
    for k, st in enumerate((start, nxt)):
        lc = pltpu.make_async_copy(
            st.at[:, own_heads], stage.at[k, c, :, pl.ds(0, HH)], in_sem.at[k]
        )
        lc.start()
        locals_in.append(lc)
    token_pairs = ((queries, xq), (gout, xo), (keys, xk), (values, xv))
    for k, (src, dst) in enumerate(token_pairs):
        lc = pltpu.make_async_copy(src.at[:, own_cols], dst.at[0:tokens], in_sem.at[2 + k])
        lc.start()
        locals_in.append(lc)

    barrier = pltpu.get_barrier_semaphore()
    near = [right, left, partner]
    if not merged:
        near = near + [xright, xleft]
    for peer in near:
        pl.semaphore_signal(barrier, inc=1, device_id=peer, device_id_type=MESH)
    if merged:

        def greet(k, carry):
            pl.semaphore_signal(
                barrier, inc=1, device_id={"dp": lax.rem(me + k, n_dp)}, device_id_type=MESH
            )
            return carry

        lax.fori_loop(1, n_dp, greet, 0)
        pl.semaphore_wait(barrier, len(near) + n_dp - 1)
    else:
        pl.semaphore_wait(barrier, len(near))

    sends = []

    def remote(src, dst, ssem, rsem, peer):
        cp = pltpu.make_async_remote_copy(
            src_ref=src, dst_ref=dst, send_sem=ssem, recv_sem=rsem,
            device_id=peer, device_id_type=MESH,
        )
        cp.start()
        sends.append(cp)
        return cp

    remotes_in = []
    for k, st in enumerate((start, nxt)):
        remotes_in.append(
            remote(
                st.at[:, other_heads], stage.at[k, c, :, pl.ds(0, HH)],
                x_ssem.at[k], x_rsem.at[k], partner,
            )
        )
    for k, (src, dst) in enumerate(token_pairs):
        remotes_in.append(
            remote(
                src.at[:, other_cols], dst.at[tokens : 2 * tokens],
                x_ssem.at[2 + k], x_rsem.at[2 + k], partner,
            )
        )

    def rows_of(offset):
        return pl.ds(pl.multiple_of(16 * chip(offset), 16), 16)

    for cc in range(2):
        for comp in range(3):
            stage[0, cc, comp, HH] = jnp.zeros((8, F), F32)
    locals_in[0].wait()
    remotes_in[0].wait_recv()
    quarter = pl.multiple_of(8 * xi, 8)
    for i in range(8):
        m = quarter + i
        h, comp = lax.div(m, 3), lax.rem(m, 3)
        ws[m, rows_of(0), :] = jnp.concatenate(
            [stage[0, 0, comp, h], stage[0, 1, comp, h]], axis=0
        ).astype(BF16)

    counts = [8, 8, 8, 3 * HH - 24]

    def span(cnt, dr, last):
        if not last:
            return 0, cnt
        return (0, cnt // 2) if dr == 0 else (cnt // 2, cnt - cnt // 2)

    ag = {}

    def gather_step(unit, step):
        for dr, (peer, sign) in enumerate(dirs):
            if step > 1:
                ag[unit, dr, step - 1].wait_recv()
            if unit == 0:
                ref, base, cnt = ws, quarter, 8
                sems = st_ssem.at[dr, step - 1], st_rsem.at[dr, step - 1]
            else:
                ref, base, cnt = wn, 8 * (unit - 1), counts[unit - 1]
                sems = ag_ssem.at[unit - 1, dr, step - 1], ag_rsem.at[unit - 1, dr, step - 1]
            lo, n = span(cnt, dr, step == far)
            piece = ref.at[pl.ds(base + lo, n), rows_of(-sign * (step - 1)), :]
            ag[unit, dr, step] = remote(piece, piece, sems[0], sems[1], peer)

    gather_step(0, 1)
    locals_in[1].wait()
    remotes_in[1].wait_recv()
    for p in range(PARTS):
        for i in range(counts[p]):
            m = 8 * p + i
            h, comp = m // 3, m % 3
            wn[m, rows_of(0), :] = jnp.concatenate(
                [stage[1, 0, comp, h], stage[1, 1, comp, h]], axis=0
            ).astype(BF16)
        gather_step(1 + p, 1)
    for step in range(2, far + 1):
        for unit in range(1 + PARTS):
            gather_step(unit, step)

    sx = {}

    def xgather(i, step):
        for dr, (peer, sign) in enumerate(xdirs):
            lo, n = 4 * i, 4
            if step == 2:
                sx[i, dr, 1].wait_recv()
                lo, n = (4 * i, 2) if dr == 0 else (4 * i + 2, 2)
            base = pl.multiple_of(8 * xpos(-sign * (step - 1)), 8)
            piece = ws.at[pl.ds(base + lo, n)]
            sx[i, dr, step] = remote(
                piece, piece, sx_ssem.at[i, dr, step - 1], sx_rsem.at[i, dr, step - 1], peer
            )

    ag[0, 0, far].wait_recv()
    ag[0, 1, far].wait_recv()
    xgather(0, 1)
    xgather(1, 1)

    def phi(h, xs, ys, w):
        cols = pl.ds(pl.multiple_of(h * D, 128), D)
        x, y = xs[:, cols], ys[:, cols]
        gu = mm(x, jnp.concatenate([w[3 * h], w[3 * h + 1]], axis=1))
        proj = mm(y, w[3 * h + 2])
        gate, up = gu[:, :F], gu[:, F:]
        s = jax.nn.sigmoid(gate)
        swish = gate * s
        hidden = (swish * up).astype(BF16)
        d_gate = (proj * up * s * (1.0 + gate * (1.0 - s))).astype(BF16)
        d_up = (proj * swish).astype(BF16)
        gab = mm_tn(x, jnp.concatenate([d_gate, d_up], axis=1))
        gc = mm_tn(y, hidden)
        return gate, up, proj, hidden, d_gate, d_up, (gab[:, :F], gab[:, F:], gc)

    def phi_a(h, carry):
        gate, up, proj, hidden, d_gate, d_up, grads = phi(h, xk, xv, ws)
        act[h, 0] = gate
        act[h, 1] = up
        act[h, 2] = proj
        rnd[h, 0] = d_gate
        rnd[h, 1] = d_up
        rnd[h, 2] = hidden
        for i in range(3):
            gbuf[3 * h + i] = grads[i].astype(BF16)
        return carry

    def phi_b(h, carry):
        grads = phi(h, xq, xo, wn)[-1]
        for i in range(3):
            psum[3 * h + i] = grads[i]
            sbuf[3 * h + i] = grads[i].astype(BF16)
        return carry

    for pad in (3 * HH, 3 * HH + 1):
        gbuf[pad] = jnp.zeros((D, F), BF16)
        sbuf[pad] = jnp.zeros((D, F), BF16)

    bufs = (gbuf, sbuf)
    rs = {}
    rows_half = D // 2

    def rs_step(k, p, step):
        for dr, (peer, sign) in enumerate(dirs):
            slot = 8 * p + chip(sign * (far + 1 - step))
            lo, n = (0, D)
            if step == 1:
                lo, n = (0, rows_half) if dr == 0 else (rows_half, rows_half)
                src = bufs[k].at[slot, pl.ds(lo, n)]
            else:
                rs[k, p, dr, step - 1].wait_recv()
                if step == 2:
                    a = 0 if dr == 0 else rows_half
                    b = rows_half - a
                    part_sum = bufs[k][slot, a : a + rows_half].astype(F32) + rs_recv[
                        k, p, dr, 0, a : a + rows_half
                    ].astype(F32)
                    rs_send[k, p, dr, 0, a : a + rows_half] = part_sum.astype(BF16)
                    rs_send[k, p, dr, 0, b : b + rows_half] = bufs[k][slot, b : b + rows_half]
                else:
                    total = bufs[k][slot].astype(F32) + rs_recv[k, p, dr, step - 2].astype(F32)
                    rs_send[k, p, dr, step - 2] = total.astype(BF16)
                src = rs_send.at[k, p, dr, step - 2]
            dst = rs_recv.at[k, p, dr, step - 1, pl.ds(lo, n)]
            rs[k, p, dr, step] = remote(
                src, dst, rs_ssem.at[k, p, dr, step - 1], rs_rsem.at[k, p, dr, step - 1], peer
            )

    def rs_total(k):
        out = []
        for p in range(PARTS):
            v = bufs[k][8 * p + z].astype(F32)
            for dr in range(2):
                rs[k, p, dr, far].wait_recv()
                v = v + rs_recv[k, p, dr, far - 1].astype(F32)
            out.append(v)
        return out

    groups = ((0, 3), (3, 6), (6, 8), (8, HH))
    for k in range(2):
        locals_in[2 + k].wait()
        remotes_in[2 + k].wait_recv()
    for p in range(PARTS):
        for unit in ((1, 2), (3,), (), (4,))[p]:
            ag[unit, 0, far].wait_recv()
            ag[unit, 1, far].wait_recv()
        lax.fori_loop(groups[p][0], groups[p][1], phi_b, 0)
        rs_step(1, p, 1)
    xgather(0, 2)
    for p in range(PARTS):
        rs_step(1, p, 2)
    xgather(1, 2)
    for step in range(3, far + 1):
        for p in range(PARTS):
            rs_step(1, p, step)
    for i in range(2):
        sx[i, 0, 2].wait_recv()
        sx[i, 1, 2].wait_recv()
    for k in range(2):
        locals_in[4 + k].wait()
        remotes_in[4 + k].wait_recv()
    for p in range(PARTS):
        lax.fori_loop(groups[p][0], groups[p][1], phi_a, 0)
        rs_step(0, p, 1)
    cts = [(RATE * v).astype(BF16) for v in rs_total(1)]
    for step in range(2, far + 1):
        for p in range(PARTS):
            rs_step(0, p, step)
    saved = newton_forward(rs_total(0))
    fields = newton_backward(saved, cts)

    fd = {}

    def field_step(p, step):
        for dr, (peer, sign) in enumerate(dirs):
            if step > 1:
                fd[p, dr, step - 1].wait_recv()
            lo, n = span(D, dr, step == far)
            piece = field.at[8 * p + chip(-sign * (step - 1)), pl.ds(lo, n)]
            fd[p, dr, step] = remote(
                piece, piece, f_ssem.at[p, dr, step - 1], f_rsem.at[p, dr, step - 1], peer
            )

    for p in range(PARTS):
        field[8 * p + z] = fields[p].astype(BF16)
        field_step(p, 1)
    for step in range(2, far + 1):
        for p in range(PARTS):
            field_step(p, step)

    def back(h, carry):
        cols = pl.ds(pl.multiple_of(h * D, 128), D)
        x, y = xk[:, cols], xv[:, cols]
        gate, up, proj = act[h, 0], act[h, 1], act[h, 2]
        d_gate, d_up, hidden = rnd[h, 0], rnd[h, 1], rnd[h, 2]
        da, db, dc = field[3 * h], field[3 * h + 1], field[3 * h + 2]
        dab = jnp.concatenate([da, db], axis=1)
        ct_gu = mm(x, dab).astype(BF16).astype(F32)
        ct_dg, ct_du = ct_gu[:, :F], ct_gu[:, F:]
        ct_h = mm(y, dc).astype(BF16).astype(F32)
        s = jax.nn.sigmoid(gate)
        swish = gate * s
        sd = s * (1.0 - s)
        q = s + gate * sd
        qd = sd * (2.0 + gate * (1.0 - 2.0 * s))
        ct_w = ct_h * up + ct_du * proj
        cq = ct_dg * q
        ct_up = (ct_h * swish + cq * proj).astype(BF16)
        ct_p = (ct_du * swish + cq * up).astype(BF16)
        ct_gate = (ct_w * q + ct_dg * (proj * up) * qd).astype(BF16)
        wab = jnp.concatenate([ws[3 * h], ws[3 * h + 1]], axis=1)
        ct_ab = jnp.concatenate([ct_gate, ct_up], axis=1)
        d_ab = jnp.concatenate([d_gate, d_up], axis=1)
        dx = mm_nt(d_ab, dab) + mm_nt(ct_ab, wab)
        dy = mm_nt(hidden, dc) + mm_nt(ct_p, ws[3 * h + 2])
        dk[:, cols] = dx.astype(BF16)
        dv[:, cols] = dy.astype(BF16)
        wg = mm_tn(x, ct_ab)
        tot[3 * h] = (psum[3 * h] + wg[:, :F]).astype(BF16)
        tot[3 * h + 1] = (psum[3 * h + 1] + wg[:, F:]).astype(BF16)
        tot[3 * h + 2] = (psum[3 * h + 2] + mm_tn(y, ct_p)).astype(BF16)
        return carry

    gr = {}

    def grad_step(p, step):
        cnt = counts[p]
        for dr, (peer, sign) in enumerate(dirs):
            rows = rows_of(sign * (far + 1 - step))
            lo, n = span(cnt, dr, step == 1)
            if step == 1:
                src = tot.at[pl.ds(8 * p + lo, n), rows, :]
            else:
                gr[p, dr, step - 1].wait_recv()
                if step == 2:
                    a, na = span(cnt, dr, True)
                    b, nb = span(cnt, 1 - dr, True)
                    own = tot[8 * p + a : 8 * p + a + na, rows, :].astype(F32)
                    own = own + gr_recv[p, dr, 0, a : a + na].astype(F32)
                    gr_send[p, dr, 0, a : a + na] = own.astype(BF16)
                    gr_send[p, dr, 0, b : b + nb] = tot[8 * p + b : 8 * p + b + nb, rows, :]
                else:
                    own = tot[8 * p : 8 * p + cnt, rows, :].astype(F32)
                    own = own + gr_recv[p, dr, step - 2, :cnt].astype(F32)
                    gr_send[p, dr, step - 2, :cnt] = own.astype(BF16)
                src = gr_send.at[p, dr, step - 2, pl.ds(0, cnt)]
            dst = gr_recv.at[p, dr, step - 1, pl.ds(lo, n)]
            gr[p, dr, step] = remote(
                src, dst, gr_ssem.at[p, dr, step - 1], gr_rsem.at[p, dr, step - 1], peer
            )

    for p in range(PARTS):
        for unit in ((0, 1), (2,), (), (3,))[p]:
            fd[unit, 0, far].wait_recv()
            fd[unit, 1, far].wait_recv()
        lax.fori_loop(groups[p][0], groups[p][1], back, 0)
        grad_step(p, 1)

    outs = []
    for k, (src, dst) in enumerate(((dk, dk_out), (dv, dv_out))):
        cp = remote(
            src.at[tokens : 2 * tokens], dst.at[:, own_cols], o_ssem.at[k], o_rsem.at[k], partner
        )
        lc = pltpu.make_async_copy(src.at[0:tokens], dst.at[:, own_cols], o_sem.at[k])
        lc.start()
        outs.append((cp, lc))

    for step in range(2, far + 1):
        for p in range(PARTS):
            grad_step(p, step)
    for p in range(PARTS):
        cnt = counts[p]
        own = tot[8 * p : 8 * p + cnt, rows_of(0), :].astype(F32)
        for dr in range(2):
            gr[p, dr, far].wait_recv()
            own = own + gr_recv[p, dr, far - 1, :cnt].astype(F32)
        part[8 * p : 8 * p + cnt] = own.astype(BF16)
    part[3 * HH :] = jnp.zeros((32 - 3 * HH, 16, F), BF16)
    if merged:
        dp_phase(n_dp, grad_out, *dp_refs)

    for cp in sends:
        cp.wait_send()
    for cp, lc in outs:
        cp.wait_recv()
        lc.wait()


def dp_phase(n, out, part, land, fin, rowbuf, swap, s1, r1, s2, r2, c_ssem, c_rsem):
    ctx = lax.axis_index("ctx")
    c = lax.rem(ctx, 2)
    other = 1 - c
    partner = ctx + 1 - 2 * c
    me = lax.axis_index("dp")
    per = 32 // n

    def scatter(k):
        j = lax.rem(me + k, n)
        return pltpu.make_async_remote_copy(
            src_ref=part.at[pl.ds(per * j, per)], dst_ref=land.at[k],
            send_sem=s1.at[k], recv_sem=r1.at[k],
            device_id={"dp": j}, device_id_type=MESH,
        )

    def spread(k):
        j = lax.rem(me + k, n)
        mine = fin.at[pl.ds(per * me, per)]
        return pltpu.make_async_remote_copy(
            src_ref=mine, dst_ref=mine, send_sem=s2.at[k], recv_sem=r2.at[k],
            device_id={"dp": j}, device_id_type=MESH,
        )

    def start1(k, carry):
        scatter(k).start()
        return carry

    def wait1(k, total):
        scatter(k).wait_recv()
        return total + land[k].astype(F32)

    lax.fori_loop(1, n, start1, 0)
    total = lax.fori_loop(1, n, wait1, part[pl.ds(per * me, per)].astype(F32)) / n
    rowbuf[0] = total[:, :8]
    rowbuf[1] = total[:, 8:]
    cp = pltpu.make_async_remote_copy(
        src_ref=rowbuf.at[other], dst_ref=swap.at[c], send_sem=c_ssem, recv_sem=c_rsem,
        device_id={"ctx": partner}, device_id_type=MESH,
    )
    cp.start()
    swap[c] = rowbuf[c]
    cp.wait_recv()
    fin[pl.ds(per * me, per)] = jnp.concatenate([swap[0], swap[1]], axis=1).astype(BF16)

    def start2(k, carry):
        spread(k).start()
        return carry

    def wait2(k, carry):
        spread(k).wait_recv()
        return carry

    lax.fori_loop(1, n, start2, 0)
    lax.fori_loop(1, n, wait2, 0)
    for h in range(HH):
        for comp in range(3):
            rows = fin[3 * h + comp].astype(F32)
            out[comp, h] = rows[:8]
            out[comp, HH + h] = rows[8:]

    def wait_sent(k, carry):
        scatter(k).wait_send()
        spread(k).wait_send()
        return carry

    lax.fori_loop(1, n, wait_sent, 0)
    cp.wait_send()


def dp_kernel(n, part, out, *refs):
    ctx = lax.axis_index("ctx")
    partner = ctx + 1 - 2 * lax.rem(ctx, 2)
    me = lax.axis_index("dp")
    barrier = pltpu.get_barrier_semaphore()

    def greet(k, carry):
        pl.semaphore_signal(
            barrier, inc=1, device_id={"dp": lax.rem(me + k, n)}, device_id_type=MESH
        )
        return carry

    lax.fori_loop(1, n, greet, 0)
    pl.semaphore_signal(barrier, inc=1, device_id={"ctx": partner}, device_id_type=MESH)
    pl.semaphore_wait(barrier, n)
    dp_phase(n, out, part, *refs)


def land_kernel(dk, dv, gs, dk_out, dv_out, gs_out, sems):
    copies = []
    for i, (src, dst) in enumerate(((dk, dk_out), (dv, dv_out), (gs, gs_out))):
        cp = pltpu.make_async_copy(src, dst, sems.at[i])
        cp.start()
        copies.append(cp)
    for cp in copies:
        cp.wait()


def dp_scratch(n_dp):
    dma = pltpu.SemaphoreType.DMA
    per = 32 // n_dp
    return [
        pltpu.VMEM((n_dp, per, 16, F), BF16),
        pltpu.VMEM((32, 16, F), BF16),
        pltpu.VMEM((2, per, 8, F), F32),
        pltpu.VMEM((2, per, 8, F), F32),
        dma((n_dp,)),
        dma((n_dp,)),
        dma((n_dp,)),
        dma((n_dp,)),
        dma,
        dma,
    ]


def run(n_dp, n_ctx, merged, keys_a, values_a, queries_b, grad_out, state_start, state_next):
    tokens = keys_a.shape[1]
    nz = n_ctx // 2
    far = nz // 2
    anyspace = pl.BlockSpec(memory_space=pl.ANY)
    vm = pl.BlockSpec(memory_space=pltpu.VMEM)
    flat = (tokens, H * D)
    dma = pltpu.SemaphoreType.DMA
    rows2 = 2 * tokens
    half = HH * D
    token_buf = pltpu.VMEM((rows2, half), BF16)
    mats = pltpu.VMEM((32, D, F), BF16)
    grad_shape = jax.ShapeDtypeStruct((3, H, 8, F), F32)
    part_shape = jax.ShapeDtypeStruct((32, 16, F), BF16)
    dp_list = dp_scratch(n_dp)
    ring_sems = [dma((PARTS, 2, far)), dma((PARTS, 2, far))]
    outs = pl.pallas_call(
        functools.partial(main_kernel, nz, n_dp // NX, n_dp, merged),
        out_shape=(
            jax.ShapeDtypeStruct(flat, BF16),
            jax.ShapeDtypeStruct(flat, BF16),
            grad_shape if merged else part_shape,
        ),
        in_specs=[pl.BlockSpec(memory_space=pltpu.HBM)] * 6,
        out_specs=(OUT_SPACE, OUT_SPACE, vm),
        scratch_shapes=([pltpu.VMEM((32, 16, F), BF16)] + dp_list if merged else [])
        + [
            token_buf, token_buf, token_buf, token_buf,
            pltpu.VMEM((2, 2, 3, HH + 1, 8, F), F32),
            mats, mats, mats, mats,
            pltpu.VMEM((3 * HH, D, F), F32),
            pltpu.VMEM((2, PARTS, 2, far - 1, D, F), BF16),
            pltpu.VMEM((2, PARTS, 2, far, D, F), BF16),
            mats,
            pltpu.VMEM((HH, 3, rows2, F), F32),
            pltpu.VMEM((HH, 3, rows2, F), BF16),
            token_buf, token_buf,
            mats,
            pltpu.VMEM((PARTS, 2, far - 1, 8, 16, F), BF16),
            pltpu.VMEM((PARTS, 2, far, 8, 16, F), BF16),
            dma((6,)), dma((6,)), dma((6,)),
            dma((2, far)), dma((2, far)),
            dma((2, 2, 2)), dma((2, 2, 2)),
        ]
        + ring_sems
        + [dma((2, PARTS, 2, far)), dma((2, PARTS, 2, far))]
        + ring_sems
        + ring_sems
        + [dma((2,)), dma((2,)), dma((2,))],
        compiler_params=pltpu.CompilerParams(
            collective_id=0, has_side_effects=True, vmem_limit_bytes=RING_VMEM
        ),
        name="ttt_ring",
    )(
        keys_a.reshape(flat),
        values_a.reshape(flat),
        queries_b.reshape(flat),
        grad_out.reshape(flat),
        state_start,
        state_next[0],
    )
    if merged:
        dk, dv, gs = outs
    else:
        dk, dv, part = outs
        gs = pl.pallas_call(
            functools.partial(dp_kernel, n_dp),
            out_shape=grad_shape,
            in_specs=[vm],
            out_specs=vm,
            scratch_shapes=dp_list,
            compiler_params=pltpu.CompilerParams(
                collective_id=1, has_side_effects=True, vmem_limit_bytes=4 * 1024 * 1024
            ),
            name="dp_sum",
        )(part)
    dk, dv, gs = pl.pallas_call(
        land_kernel,
        out_shape=(
            jax.ShapeDtypeStruct(flat, BF16),
            jax.ShapeDtypeStruct(flat, BF16),
            grad_shape,
        ),
        in_specs=[vm] * 3,
        out_specs=(anyspace,) * 3,
        scratch_shapes=[dma((3,))],
        compiler_params=pltpu.CompilerParams(vmem_limit_bytes=8 * 1024 * 1024),
        name="land",
    )(dk, dv, gs)
    return dk.reshape(keys_a.shape), dv.reshape(keys_a.shape), gs


MERGED = True
OUT_SPACE = pl.BlockSpec(memory_space=pltpu.VMEM)
RING_VMEM = 53000 * 1024


def solution(mesh):
    placed = (
        P("dp", "ctx", None),
        P("dp", "ctx", None),
        P("dp", "ctx", None),
        P("dp", "ctx", None),
        P(None, None, "ctx", None),
        P("dp", None, None, "ctx", None),
    )
    return jax.shard_map(
        functools.partial(run, mesh.shape["dp"], mesh.shape["ctx"], MERGED),
        mesh=mesh,
        in_specs=placed,
        out_specs=(P("dp", "ctx", None), P("dp", "ctx", None), P(None, None, "ctx", None)),
        check_vma=False,
    )
```

time: 142 us -> 120 us (0.85)
  Pallas kernels: 137 us -> 118 us
  local copies, waits for them, and re-layouts: 3.91 us -> 1.88 us
    pallas_call x2, Pallas kernels: 137 us -> 118 us  [the longest x1 116 us: run(): pl.pallas_call(functools.partial(main_kernel, nz, n_dp // NX, n_dp, merge...]
    unnamed x7 -> x4, local copies, waits for them, and re-layouts: 3.91 us -> 1.88 us
where the time goes in v2:
time: 120 us
  Pallas kernels  118 us (98%)
  local copies, waits for them, and re-layouts  1.88 us (2%)
    pallas_call x1, Pallas kernels, run(): pl.pallas_call(functools.partial(main_kernel, nz, n_dp // NX, n_dp, merge...  116 us

profile of v2, /device:TPU:1, one launch (start us, length us, event | category | flops | bytes accessed | tf_op | source)
XLA Modules:
  0.0 120.2 jit_solution(10365659598069256257)
XLA Ops:
  0.6 0.0 copy-start
  0.6 0.9 copy-done
  1.6 0.0 copy-start.1
  1.6 0.9 copy-done.1
  2.5 116.5 %ttt_ring.1 = (bf16[128,2560]{1,0:T(8,128)(2,1)S(1)}, bf16[128,2560]{1,0:T(8,128)(2,1)S(1)}, f32[3,20,8,128]{3,2,1,0:T(8,128)S(1)}) custom-call(bf16[128,2560]{1,0:T(8,128)(2,1)} %bitcast.8, bf16[128,2560]{1,0:T(8,128)(2,1)} %bitcast.9, bf16[128,2560]{1,0:T(8,128)(2,1)} %bitcast.10, bf16[128,2560]{1,0:T(8,128)(2,1)} %bitcast.11, ...), custom_call_target="tpu_custom_call" | custom-call | tf_op jit(solution)/shard_map/ttt_ring/pallas_call | solution.py:623
  119.0 1.2 land.1
Async XLA Ops:
  0.6 0.9 copy-start
  1.6 0.9 copy-start.1

commit v3 on v2

--- a/solution.py
+++ b/solution.py
@@ -81,21 +81,16 @@
 
 
 def main_kernel(
-    nz, ny, n_dp, merged,
+    nz, ny, n_dp,
     keys, values, queries, gout, start, nxt,
     *refs,
 ):
-    if merged:
-        dk_out, dv_out, grad_out = refs[:3]
-        refs = refs[3:]
-        dp_refs, refs = refs[:11], refs[11:]
-        part = dp_refs[0]
-    else:
-        dk_out, dv_out, part = refs[:3]
-        refs = refs[3:]
+    dk_out, dv_out, grad_out = refs[:3]
+    dp_refs, refs = refs[3:10], refs[10:]
+    part = dp_refs[0]
     (
         xk, xv, xq, xo, stage, ws, wn, gbuf, sbuf, psum,
-        rs_send, rs_recv, field, act, rnd, dk, dv, tot, gr_send, gr_recv,
+        rs_send, rs_recv, field, act, aux, rnd, dk, dv, tot, gr_send, gr_recv,
         in_sem, x_ssem, x_rsem, st_ssem, st_rsem, sx_ssem, sx_rsem, ag_ssem, ag_rsem,
         rs_ssem, rs_rsem, f_ssem, f_rsem, gr_ssem, gr_rsem, o_sem, o_ssem, o_rsem,
     ) = refs
@@ -143,23 +138,20 @@
         locals_in.append(lc)
 
     barrier = pltpu.get_barrier_semaphore()
-    near = [right, left, partner]
-    if not merged:
-        near = near + [xright, xleft]
+    near = (right, left, partner)
     for peer in near:
         pl.semaphore_signal(barrier, inc=1, device_id=peer, device_id_type=MESH)
-    if merged:
-
-        def greet(k, carry):
+
+    def greet(k, carry):
+        for r in range(2):
             pl.semaphore_signal(
-                barrier, inc=1, device_id={"dp": lax.rem(me + k, n_dp)}, device_id_type=MESH
+                barrier, inc=1,
+                device_id={"dp": lax.rem(me + k, n_dp), "ctx": 2 * z + r}, device_id_type=MESH,
             )
-            return carry
-
-        lax.fori_loop(1, n_dp, greet, 0)
-        pl.semaphore_wait(barrier, len(near) + n_dp - 1)
-    else:
-        pl.semaphore_wait(barrier, len(near))
+        return carry
+
+    lax.fori_loop(1, n_dp, greet, 0)
+    pl.semaphore_wait(barrier, len(near) + 2 * (n_dp - 1))
 
     sends = []
 
@@ -262,7 +254,7 @@
     xgather(1, 1)
 
     def phi(h, xs, ys, w):
-        cols = pl.ds(pl.multiple_of(h * D, 128), D)
+        cols = slice(h * D, (h + 1) * D)
         x, y = xs[:, cols], ys[:, cols]
         gu = mm(x, jnp.concatenate([w[3 * h], w[3 * h + 1]], axis=1))
         proj = mm(y, w[3 * h + 2])
@@ -276,7 +268,7 @@
         gc = mm_tn(y, hidden)
         return gate, up, proj, hidden, d_gate, d_up, (gab[:, :F], gab[:, F:], gc)
 
-    def phi_a(h, carry):
+    def phi_a(h):
         gate, up, proj, hidden, d_gate, d_up, grads = phi(h, xk, xv, ws)
         act[h, 0] = gate
         act[h, 1] = up
@@ -286,14 +278,12 @@
         rnd[h, 2] = hidden
         for i in range(3):
             gbuf[3 * h + i] = grads[i].astype(BF16)
-        return carry
-
-    def phi_b(h, carry):
+
+    def phi_b(h):
         grads = phi(h, xq, xo, wn)[-1]
         for i in range(3):
             psum[3 * h + i] = grads[i]
             sbuf[3 * h + i] = grads[i].astype(BF16)
-        return carry
 
     for pad in (3 * HH, 3 * HH + 1):
         gbuf[pad] = jnp.zeros((D, F), BF16)
@@ -329,9 +319,9 @@
                 src, dst, rs_ssem.at[k, p, dr, step - 1], rs_rsem.at[k, p, dr, step - 1], peer
             )
 
-    def rs_total(k):
+    def rs_total(k, parts):
         out = []
-        for p in range(PARTS):
+        for p in parts:
             v = bufs[k][8 * p + z].astype(F32)
             for dr in range(2):
                 rs[k, p, dr, far].wait_recv()
@@ -347,7 +337,8 @@
         for unit in ((1, 2), (3,), (), (4,))[p]:
             ag[unit, 0, far].wait_recv()
             ag[unit, 1, far].wait_recv()
-        lax.fori_loop(groups[p][0], groups[p][1], phi_b, 0)
+        for h in range(groups[p][0], groups[p][1]):
+            phi_b(h)
         rs_step(1, p, 1)
     xgather(0, 2)
     for p in range(PARTS):
@@ -363,15 +354,13 @@
         locals_in[4 + k].wait()
         remotes_in[4 + k].wait_recv()
     for p in range(PARTS):
-        lax.fori_loop(groups[p][0], groups[p][1], phi_a, 0)
+        for h in range(groups[p][0], groups[p][1]):
+            phi_a(h)
         rs_step(0, p, 1)
-    cts = [(RATE * v).astype(BF16) for v in rs_total(1)]
+    cts = [(RATE * v).astype(BF16) for v in rs_total(1, range(PARTS))]
     for step in range(2, far + 1):
         for p in range(PARTS):
             rs_step(0, p, step)
-    saved = newton_forward(rs_total(0))
-    fields = newton_backward(saved, cts)
-
     fd = {}
 
     def field_step(p, step):
@@ -384,33 +373,43 @@
                 piece, piece, f_ssem.at[p, dr, step - 1], f_rsem.at[p, dr, step - 1], peer
             )
 
-    for p in range(PARTS):
-        field[8 * p + z] = fields[p].astype(BF16)
-        field_step(p, 1)
+    for pair in ((0, 1), (2, 3)):
+        saved = newton_forward(rs_total(0, pair))
+        fields = newton_backward(saved, [cts[p] for p in pair])
+        for p, value in zip(pair, fields):
+            field[8 * p + z] = value.astype(BF16)
+            field_step(p, 1)
+
+    def ready(h):
+        gate, up, proj = act[h, 0], act[h, 1], act[h, 2]
+        s = jax.nn.sigmoid(gate)
+        sd = s * (1.0 - s)
+        aux[h, 0] = gate * s
+        aux[h, 1] = s + gate * sd
+        aux[h, 2] = (proj * up) * (sd * (2.0 + gate * (1.0 - 2.0 * s)))
+
     for step in range(2, far + 1):
+        for h in range(HH * (step - 2) // (far - 1), HH * (step - 1) // (far - 1)):
+            ready(h)
         for p in range(PARTS):
             field_step(p, step)
 
-    def back(h, carry):
-        cols = pl.ds(pl.multiple_of(h * D, 128), D)
+    def back(h):
+        cols = slice(h * D, (h + 1) * D)
         x, y = xk[:, cols], xv[:, cols]
-        gate, up, proj = act[h, 0], act[h, 1], act[h, 2]
+        up, proj = act[h, 1], act[h, 2]
+        swish, q, bend = aux[h, 0], aux[h, 1], aux[h, 2]
         d_gate, d_up, hidden = rnd[h, 0], rnd[h, 1], rnd[h, 2]
         da, db, dc = field[3 * h], field[3 * h + 1], field[3 * h + 2]
         dab = jnp.concatenate([da, db], axis=1)
         ct_gu = mm(x, dab).astype(BF16).astype(F32)
         ct_dg, ct_du = ct_gu[:, :F], ct_gu[:, F:]
         ct_h = mm(y, dc).astype(BF16).astype(F32)
-        s = jax.nn.sigmoid(gate)
-        swish = gate * s
-        sd = s * (1.0 - s)
-        q = s + gate * sd
-        qd = sd * (2.0 + gate * (1.0 - 2.0 * s))
         ct_w = ct_h * up + ct_du * proj
         cq = ct_dg * q
         ct_up = (ct_h * swish + cq * proj).astype(BF16)
         ct_p = (ct_du * swish + cq * up).astype(BF16)
-        ct_gate = (ct_w * q + ct_dg * (proj * up) * qd).astype(BF16)
+        ct_gate = (ct_w * q + ct_dg * bend).astype(BF16)
         wab = jnp.concatenate([ws[3 * h], ws[3 * h + 1]], axis=1)
         ct_ab = jnp.concatenate([ct_gate, ct_up], axis=1)
         d_ab = jnp.concatenate([d_gate, d_up], axis=1)
@@ -422,7 +421,6 @@
         tot[3 * h] = (psum[3 * h] + wg[:, :F]).astype(BF16)
         tot[3 * h + 1] = (psum[3 * h + 1] + wg[:, F:]).astype(BF16)
         tot[3 * h + 2] = (psum[3 * h + 2] + mm_tn(y, ct_p)).astype(BF16)
-        return carry
 
     gr = {}
 
@@ -456,7 +454,8 @@
         for unit in ((0, 1), (2,), (), (3,))[p]:
             fd[unit, 0, far].wait_recv()
             fd[unit, 1, far].wait_recv()
-        lax.fori_loop(groups[p][0], groups[p][1], back, 0)
+        for h in range(groups[p][0], groups[p][1]):
+            back(h)
         grad_step(p, 1)
 
     outs = []
@@ -471,16 +470,19 @@
     for step in range(2, far + 1):
         for p in range(PARTS):
             grad_step(p, step)
+    send_rows, finish_rows = dp_phase(n_dp, z, c, me, grad_out, *dp_refs)
     for p in range(PARTS):
         cnt = counts[p]
         own = tot[8 * p : 8 * p + cnt, rows_of(0), :].astype(F32)
         for dr in range(2):
             gr[p, dr, far].wait_recv()
             own = own + gr_recv[p, dr, far - 1, :cnt].astype(F32)
-        part[8 * p : 8 * p + cnt] = own.astype(BF16)
-    part[3 * HH :] = jnp.zeros((32 - 3 * HH, 16, F), BF16)
-    if merged:
-        dp_phase(n_dp, grad_out, *dp_refs)
+        part[0, 8 * p : 8 * p + cnt] = own[:, :8]
+        part[1, 8 * p : 8 * p + cnt] = own[:, 8:]
+        if cnt < 8:
+            part[:, 8 * p + cnt : 8 * p + 8] = jnp.zeros((2, 8 - cnt, 8, F), F32)
+        send_rows(p)
+    finish_rows()
 
     for cp in sends:
         cp.wait_send()
@@ -489,20 +491,22 @@
         lc.wait()
 
 
-def dp_phase(n, out, part, land, fin, rowbuf, swap, s1, r1, s2, r2, c_ssem, c_rsem):
-    ctx = lax.axis_index("ctx")
-    c = lax.rem(ctx, 2)
+def dp_phase(n, z, c, me, out, part, land, fin, s1, r1, s2, r2):
+    per = 32 // n
     other = 1 - c
-    partner = ctx + 1 - 2 * c
-    me = lax.axis_index("dp")
-    per = 32 // n
-
-    def scatter(k):
-        j = lax.rem(me + k, n)
+
+    def rows_to(j, r):
         return pltpu.make_async_remote_copy(
-            src_ref=part.at[pl.ds(per * j, per)], dst_ref=land.at[k],
-            send_sem=s1.at[k], recv_sem=r1.at[k],
-            device_id={"dp": j}, device_id_type=MESH,
+            src_ref=part.at[r, pl.ds(per * j, per)], dst_ref=land.at[me, c],
+            send_sem=s1.at[j, r], recv_sem=r1.at[me, c],
+            device_id={"dp": j, "ctx": 2 * z + r}, device_id_type=MESH,
+        )
+
+    def rows_from(j, core):
+        return pltpu.make_async_remote_copy(
+            src_ref=part.at[0, pl.ds(0, per)], dst_ref=land.at[j, core],
+            send_sem=s1.at[j, core], recv_sem=r1.at[j, core],
+            device_id={"dp": j, "ctx": 2 * z + core}, device_id_type=MESH,
         )
 
     def spread(k):
@@ -513,77 +517,70 @@
             device_id={"dp": j}, device_id_type=MESH,
         )
 
-    def start1(k, carry):
-        scatter(k).start()
-        return carry
-
-    def wait1(k, total):
-        scatter(k).wait_recv()
-        return total + land[k].astype(F32)
-
-    lax.fori_loop(1, n, start1, 0)
-    total = lax.fori_loop(1, n, wait1, part[pl.ds(per * me, per)].astype(F32)) / n
-    rowbuf[0] = total[:, :8]
-    rowbuf[1] = total[:, 8:]
-    cp = pltpu.make_async_remote_copy(
-        src_ref=rowbuf.at[other], dst_ref=swap.at[c], send_sem=c_ssem, recv_sem=c_rsem,
-        device_id={"ctx": partner}, device_id_type=MESH,
-    )
-    cp.start()
-    swap[c] = rowbuf[c]
-    cp.wait_recv()
-    fin[pl.ds(per * me, per)] = jnp.concatenate([swap[0], swap[1]], axis=1).astype(BF16)
-
-    def start2(k, carry):
-        spread(k).start()
-        return carry
-
-    def wait2(k, carry):
-        spread(k).wait_recv()
-        return carry
-
-    lax.fori_loop(1, n, start2, 0)
-    lax.fori_loop(1, n, wait2, 0)
-    for h in range(HH):
-        for comp in range(3):
-            rows = fin[3 * h + comp].astype(F32)
-            out[comp, h] = rows[:8]
-            out[comp, HH + h] = rows[8:]
-
-    def wait_sent(k, carry):
-        scatter(k).wait_send()
-        spread(k).wait_send()
-        return carry
-
-    lax.fori_loop(1, n, wait_sent, 0)
-    cp.wait_send()
-
-
-def dp_kernel(n, part, out, *refs):
-    ctx = lax.axis_index("ctx")
-    partner = ctx + 1 - 2 * lax.rem(ctx, 2)
-    me = lax.axis_index("dp")
-    barrier = pltpu.get_barrier_semaphore()
-
-    def greet(k, carry):
-        pl.semaphore_signal(
-            barrier, inc=1, device_id={"dp": lax.rem(me + k, n)}, device_id_type=MESH
-        )
-        return carry
-
-    lax.fori_loop(1, n, greet, 0)
-    pl.semaphore_signal(barrier, inc=1, device_id={"ctx": partner}, device_id_type=MESH)
-    pl.semaphore_wait(barrier, n)
-    dp_phase(n, out, part, *refs)
-
-
-def land_kernel(dk, dv, gs, dk_out, dv_out, gs_out, sems):
-    copies = []
-    for i, (src, dst) in enumerate(((dk, dk_out), (dv, dv_out), (gs, gs_out))):
-        cp = pltpu.make_async_copy(src, dst, sems.at[i])
+    def send_rows(p):
+        for j in range(8 * p // per, 8 * (p + 1) // per):
+            for r in range(2):
+
+                @pl.when(2 * me + c != 2 * j + r)
+                def _():
+                    rows_to(j, r).start()
+
+    def finish_rows():
+        rows_from(me, other).wait_recv()
+        own = part[c, pl.ds(per * me, per)]
+        across = land[me, other]
+        first = jnp.where(c == 0, own, across)
+        second = jnp.where(c == 0, across, own)
+
+        def take(k, carry):
+            j = lax.rem(me + k, n)
+            rows_from(j, 0).wait_recv()
+            rows_from(j, 1).wait_recv()
+            return carry[0] + land[j, 0], carry[1] + land[j, 1]
+
+        first, second = lax.fori_loop(1, n, take, (first, second))
+        both = jnp.concatenate([first, second], axis=1) / n
+        fin[pl.ds(per * me, per)] = both.astype(BF16)
+
+        def start2(k, carry):
+            spread(k).start()
+            return carry
+
+        def wait2(k, carry):
+            spread(k).wait_recv()
+            return carry
+
+        lax.fori_loop(1, n, start2, 0)
+        lax.fori_loop(1, n, wait2, 0)
+        for h in range(HH):
+            for comp in range(3):
+                rows = fin[3 * h + comp].astype(F32)
+                out[comp, h] = rows[:8]
+                out[comp, HH + h] = rows[8:]
+
+        def wait_sent(k, carry):
+            j = lax.rem(me + k, n)
+            rows_from(j, 0).wait_send()
+            rows_from(j, 1).wait_send()
+            spread(k).wait_send()
+            return carry
+
+        rows_from(me, other).wait_send()
+        lax.fori_loop(1, n, wait_sent, 0)
+
+    return send_rows, finish_rows
+
+
+def land_kernel(dk, dv, gs, dk_out, dv_out, gs_out, b0, b1, b2, in_sems, out_sems):
+    trips = ((gs, b2, gs_out), (dk, b0, dk_out), (dv, b1, dv_out))
+    loads = [pltpu.make_async_copy(t[0], t[1], in_sems.at[i]) for i, t in enumerate(trips)]
+    stores = [pltpu.make_async_copy(t[1], t[2], out_sems.at[i]) for i, t in enumerate(trips)]
+    for cp in loads:
         cp.start()
-        copies.append(cp)
-    for cp in copies:
+    for load, store in zip(loads, stores):
+        load.wait()
+        store.start()
+    for cp in stores:
         cp.wait()
 
 
@@ -591,20 +588,17 @@
     dma = pltpu.SemaphoreType.DMA
     per = 32 // n_dp
     return [
-        pltpu.VMEM((n_dp, per, 16, F), BF16),
+        pltpu.VMEM((2, 32, 8, F), F32),
+        pltpu.VMEM((n_dp, 2, per, 8, F), F32),
         pltpu.VMEM((32, 16, F), BF16),
-        pltpu.VMEM((2, per, 8, F), F32),
-        pltpu.VMEM((2, per, 8, F), F32),
+        dma((n_dp, 2)),
+        dma((n_dp, 2)),
         dma((n_dp,)),
         dma((n_dp,)),
-        dma((n_dp,)),
-        dma((n_dp,)),
-        dma,
-        dma,
     ]
 
 
-def run(n_dp, n_ctx, merged, keys_a, values_a, queries_b, grad_out, state_start, state_next):
+def run(n_dp, n_ctx, keys_a, values_a, queries_b, grad_out, state_start, state_next):
     tokens = keys_a.shape[1]
     nz = n_ctx // 2
     far = nz // 2
@@ -617,19 +611,18 @@
     token_buf = pltpu.VMEM((rows2, half), BF16)
     mats = pltpu.VMEM((32, D, F), BF16)
     grad_shape = jax.ShapeDtypeStruct((3, H, 8, F), F32)
-    part_shape = jax.ShapeDtypeStruct((32, 16, F), BF16)
     dp_list = dp_scratch(n_dp)
     ring_sems = [dma((PARTS, 2, far)), dma((PARTS, 2, far))]
     outs = pl.pallas_call(
-        functools.partial(main_kernel, nz, n_dp // NX, n_dp, merged),
+        functools.partial(main_kernel, nz, n_dp // NX, n_dp),
         out_shape=(
             jax.ShapeDtypeStruct(flat, BF16),
             jax.ShapeDtypeStruct(flat, BF16),
-            grad_shape if merged else part_shape,
+            grad_shape,
         ),
         in_specs=[pl.BlockSpec(memory_space=pltpu.HBM)] * 6,
         out_specs=(OUT_SPACE, OUT_SPACE, vm),
-        scratch_shapes=([pltpu.VMEM((32, 16, F), BF16)] + dp_list if merged else [])
+        scratch_shapes=dp_list
         + [
             token_buf, token_buf, token_buf, token_buf,
             pltpu.VMEM((2, 2, 3, HH + 1, 8, F), F32),
@@ -638,6 +631,7 @@
             pltpu.VMEM((2, PARTS, 2, far - 1, D, F), BF16),
             pltpu.VMEM((2, PARTS, 2, far, D, F), BF16),
             mats,
+            pltpu.VMEM((HH, 3, rows2, F), F32),
             pltpu.VMEM((HH, 3, rows2, F), F32),
             pltpu.VMEM((HH, 3, rows2, F), BF16),
             token_buf, token_buf,
@@ -665,21 +659,6 @@
         state_start,
         state_next[0],
     )
-    if merged:
-        dk, dv, gs = outs
-    else:
-        dk, dv, part = outs
-        gs = pl.pallas_call(
-            functools.partial(dp_kernel, n_dp),
-            out_shape=grad_shape,
-            in_specs=[vm],
-            out_specs=vm,
-            scratch_shapes=dp_list,
-            compiler_params=pltpu.CompilerParams(
-                collective_id=1, has_side_effects=True, vmem_limit_bytes=4 * 1024 * 1024
-            ),
-            name="dp_sum",
-        )(part)
     dk, dv, gs = pl.pallas_call(
         land_kernel,
         out_shape=(
@@ -687,18 +666,22 @@
             jax.ShapeDtypeStruct(flat, BF16),
             grad_shape,
         ),
-        in_specs=[vm] * 3,
+        in_specs=[LAND_SPACE] * 3,
         out_specs=(anyspace,) * 3,
-        scratch_shapes=[dma((3,))],
-        compiler_params=pltpu.CompilerParams(vmem_limit_bytes=8 * 1024 * 1024),
+        scratch_shapes=[
+            pltpu.VMEM(flat, BF16), pltpu.VMEM(flat, BF16), pltpu.VMEM((3, H, 8, F), F32),
+            dma((3,)), dma((3,)),
+        ],
+        compiler_params=pltpu.CompilerParams(vmem_limit_bytes=LAND_VMEM),
         name="land",
-    )(dk, dv, gs)
+    )(*outs)
     return dk.reshape(keys_a.shape), dv.reshape(keys_a.shape), gs
 
 
-MERGED = True
-OUT_SPACE = pl.BlockSpec(memory_space=pltpu.VMEM)
-RING_VMEM = 53000 * 1024
+OUT_SPACE = pl.BlockSpec(memory_space=pl.ANY)
+LAND_SPACE = pl.BlockSpec(memory_space=pltpu.HBM)
+RING_VMEM = 56 * 1024 * 1024
+LAND_VMEM = 56 * 1024 * 1024
 
 
 def solution(mesh):
@@ -711,7 +694,7 @@
         P("dp", None, None, "ctx", None),
     )
     return jax.shard_map(
-        functools.partial(run, mesh.shape["dp"], mesh.shape["ctx"], MERGED),
+        functools.partial(run, mesh.shape["dp"], mesh.shape["ctx"]),
         mesh=mesh,
         in_specs=placed,
         out_specs=(P("dp", "ctx", None), P("dp", "ctx", None), P(None, None, "ctx", None)),

time: 120 us -> 117 us (0.975)
  Pallas kernels: 118 us -> 116 us
  local copies, waits for them, and re-layouts: 1.88 us -> 0 us
    pallas_call x1, Pallas kernels: 116 us -> 113 us  [run(): pl.pallas_call(functools.partial(main_kernel, nz, n_dp // NX, n_dp), out_...]
    unnamed x4 -> x0, local copies, waits for them, and re-layouts: 1.88 us -> none
where the time goes in v3:
time: 117 us; the launch traced here: 116 us
  Pallas kernels  116 us (99%)
    pallas_call x1, Pallas kernels, run(): pl.pallas_call(functools.partial(main_kernel, nz, n_dp // NX, n_dp), out_...  113 us

profile of v3, /device:TPU:1, one launch (start us, length us, event | category | flops | bytes accessed | tf_op | source)
XLA Modules:
  0.0 116.4 jit_solution(12742046814068161735)
XLA Ops:
  0.6 113.4 %ttt_ring.1 = (bf16[128,2560]{1,0:T(8,128)(2,1)}, bf16[128,2560]{1,0:T(8,128)(2,1)}, f32[3,20,8,128]{3,2,1,0:T(8,128)}) custom-call(bf16[128,2560]{1,0:T(8,128)(2,1)} %bitcast.7, bf16[128,2560]{1,0:T(8,128)(2,1)} %bitcast.8, bf16[128,2560]{1,0:T(8,128)(2,1)} %bitcast.9, bf16[128,2560]{1,0:T(8,128)(2,1)} %bitcast.10, f32[3,20,8,128]{3,2,1,0:T(8,128)} %start.1, ...), custom_call_target="tpu_custom_call" | custom-call | tf_op jit(solution)/shard_map/ttt_ring/pallas_call | solution.py:616
  114.0 2.3 %land.1 = (bf16[128,2560]{1,0:T(8,128)(2,1)}, bf16[128,2560]{1,0:T(8,128)(2,1)}, f32[3,20,8,128]{3,2,1,0:T(8,128)}) custom-call(bf16[128,2560]{1,0:T(8,128)(2,1)} %get-tuple-element.9.dk, bf16[128,2560]{1,0:T(8,128)(2,1)} %get-tuple-element.10.dv, f32[3,20,8,128]{3,2,1,0:T(8,128)} %get-tuple-element.11.gs), custom_call_target="tpu_custom_call" | custom-call | tf_op jit(solution)/shard_map/land/pallas_call | solution.py:662

commit v4 on v3

--- a/solution.py
+++ b/solution.py
@@ -92,7 +92,7 @@
         xk, xv, xq, xo, stage, ws, wn, gbuf, sbuf, psum,
         rs_send, rs_recv, field, act, aux, rnd, dk, dv, tot, gr_send, gr_recv,
         in_sem, x_ssem, x_rsem, st_ssem, st_rsem, sx_ssem, sx_rsem, ag_ssem, ag_rsem,
-        rs_ssem, rs_rsem, f_ssem, f_rsem, gr_ssem, gr_rsem, o_sem, o_ssem, o_rsem,
+        rs_ssem, rs_rsem, f_ssem, f_rsem, gr_ssem, gr_rsem, o_sem, o_ssem, o_rsem, word,
     ) = refs
     ctx = lax.axis_index("ctx")
     z = lax.div(ctx, 2)
@@ -138,20 +138,19 @@
         locals_in.append(lc)
 
     barrier = pltpu.get_barrier_semaphore()
-    near = (right, left, partner)
+    around = [partner, xright, xleft]
+    if ny > 1:
+        around.append({"dp": xi * ny + lax.rem(yi + 1, ny)})
+        around.append({"dp": xi * ny + lax.rem(yi + ny - 1, ny)})
+    near = [right, left] + around
     for peer in near:
         pl.semaphore_signal(barrier, inc=1, device_id=peer, device_id_type=MESH)
-
-    def greet(k, carry):
-        for r in range(2):
-            pl.semaphore_signal(
-                barrier, inc=1,
-                device_id={"dp": lax.rem(me + k, n_dp), "ctx": 2 * z + r}, device_id_type=MESH,
-            )
-        return carry
-
-    lax.fori_loop(1, n_dp, greet, 0)
-    pl.semaphore_wait(barrier, len(near) + 2 * (n_dp - 1))
+    pl.semaphore_wait(barrier, len(near))
+
+    def pass_word(step):
+        for peer in around:
+            pl.semaphore_signal(word.at[step], inc=1, device_id=peer, device_id_type=MESH)
+        pl.semaphore_wait(word.at[step], len(around))
 
     sends = []
 
@@ -172,7 +171,9 @@
                 x_ssem.at[k], x_rsem.at[k], partner,
             )
         )
-    for k, (src, dst) in enumerate(token_pairs):
+
+    def swap_tokens(k):
+        src, dst = token_pairs[k]
         remotes_in.append(
             remote(
                 src.at[:, other_cols], dst.at[tokens : 2 * tokens],
@@ -233,6 +234,12 @@
     for step in range(2, far + 1):
         for unit in range(1 + PARTS):
             gather_step(unit, step)
+        if step == 2:
+            swap_tokens(0)
+            swap_tokens(1)
+        if step == far:
+            swap_tokens(2)
+            swap_tokens(3)
 
     sx = {}
 
@@ -252,6 +259,7 @@
     ag[0, 1, far].wait_recv()
     xgather(0, 1)
     xgather(1, 1)
+    pass_word(0)
 
     def phi(h, xs, ys, w):
         cols = slice(h * D, (h + 1) * D)
@@ -340,10 +348,12 @@
         for h in range(groups[p][0], groups[p][1]):
             phi_b(h)
         rs_step(1, p, 1)
+    pass_word(1)
     xgather(0, 2)
     for p in range(PARTS):
         rs_step(1, p, 2)
     xgather(1, 2)
+    pass_word(2)
     for step in range(3, far + 1):
         for p in range(PARTS):
             rs_step(1, p, step)
@@ -357,6 +367,7 @@
         for h in range(groups[p][0], groups[p][1]):
             phi_a(h)
         rs_step(0, p, 1)
+    pass_word(3)
     cts = [(RATE * v).astype(BF16) for v in rs_total(1, range(PARTS))]
     for step in range(2, far + 1):
         for p in range(PARTS):
@@ -373,6 +384,7 @@
                 piece, piece, f_ssem.at[p, dr, step - 1], f_rsem.at[p, dr, step - 1], peer
             )
 
+    pass_word(4)
     for pair in ((0, 1), (2, 3)):
         saved = newton_forward(rs_total(0, pair))
         fields = newton_backward(saved, [cts[p] for p in pair])
@@ -422,6 +434,8 @@
         tot[3 * h + 1] = (psum[3 * h + 1] + wg[:, F:]).astype(BF16)
         tot[3 * h + 2] = (psum[3 * h + 2] + mm_tn(y, ct_p)).astype(BF16)
 
+    pass_word(5)
+
     gr = {}
 
     def grad_step(p, step):
@@ -458,18 +472,18 @@
             back(h)
         grad_step(p, 1)
 
-    outs = []
-    for k, (src, dst) in enumerate(((dk, dk_out), (dv, dv_out))):
-        cp = remote(
-            src.at[tokens : 2 * tokens], dst.at[:, own_cols], o_ssem.at[k], o_rsem.at[k], partner
-        )
-        lc = pltpu.make_async_copy(src.at[0:tokens], dst.at[:, own_cols], o_sem.at[k])
-        lc.start()
-        outs.append((cp, lc))
-
     for step in range(2, far + 1):
         for p in range(PARTS):
             grad_step(p, step)
+        if step == far - 1:
+            outs = []
+            for k, (src, dst) in enumerate(((dk, dk_out), (dv, dv_out))):
+                cp = remote(
+                    src.at[tokens : 2 * tokens], dst.at[:, own_cols], o_ssem.at[k], o_rsem.at[k], partner
+                )
+                lc = pltpu.make_async_copy(src.at[0:tokens], dst.at[:, own_cols], o_sem.at[k])
+                lc.start()
+                outs.append((cp, lc))
     send_rows, finish_rows = dp_phase(n_dp, z, c, me, grad_out, *dp_refs)
     for p in range(PARTS):
         cnt = counts[p]
@@ -646,7 +660,7 @@
         + [dma((2, PARTS, 2, far)), dma((2, PARTS, 2, far))]
         + ring_sems
         + ring_sems
-        + [dma((2,)), dma((2,)), dma((2,))],
+        + [dma((2,)), dma((2,)), dma((2,)), pltpu.SemaphoreType.REGULAR((NX // 2 + 4,))],
         compiler_params=pltpu.CompilerParams(
             collective_id=0, has_side_effects=True, vmem_limit_bytes=RING_VMEM
         ),

time: 117 us -> 114 us (0.974)
  Pallas kernels: 116 us -> 113 us
    pallas_call x1, Pallas kernels: 113 us -> 110 us  [run(): pl.pallas_call(functools.partial(main_kernel, nz, n_dp // NX, n_dp), out_...]
where the time goes in v4:
time: 114 us; the launch traced here: 113 us
  Pallas kernels  113 us (99%)
    pallas_call x1, Pallas kernels, run(): pl.pallas_call(functools.partial(main_kernel, nz, n_dp // NX, n_dp), out_...  110 us
    pallas_call x1, Pallas kernels, run(): pl.pallas_call(land_kernel, out_shape=(jax.ShapeDtypeStruct(flat, BF16),...  2.32 us

profile of v4, /device:TPU:1, one launch (start us, length us, event | category | flops | bytes accessed | tf_op | source)
XLA Modules:
  0.0 113.3 jit_solution(17720260801783656530)
XLA Ops:
  0.6 110.3 %ttt_ring.1 = (bf16[128,2560]{1,0:T(8,128)(2,1)}, bf16[128,2560]{1,0:T(8,128)(2,1)}, f32[3,20,8,128]{3,2,1,0:T(8,128)}) custom-call(bf16[128,2560]{1,0:T(8,128)(2,1)} %bitcast.7, bf16[128,2560]{1,0:T(8,128)(2,1)} %bitcast.8, bf16[128,2560]{1,0:T(8,128)(2,1)} %bitcast.9, bf16[128,2560]{1,0:T(8,128)(2,1)} %bitcast.10, f32[3,20,8,128]{3,2,1,0:T(8,128)} %start.1, ...), custom_call_target="tpu_custom_call" | custom-call | tf_op jit(solution)/shard_map/ttt_ring/pallas_call | solution.py:630
  111.0 2.3 %land.1 = (bf16[128,2560]{1,0:T(8,128)(2,1)}, bf16[128,2560]{1,0:T(8,128)(2,1)}, f32[3,20,8,128]{3,2,1,0:T(8,128)}) custom-call(bf16[128,2560]{1,0:T(8,128)(2,1)} %get-tuple-element.9.dk, bf16[128,2560]{1,0:T(8,128)(2,1)} %get-tuple-element.10.dv, f32[3,20,8,128]{3,2,1,0:T(8,128)} %get-tuple-element.11.gs), custom_call_target="tpu_custom_call" | custom-call | tf_op jit(solution)/shard_map/land/pallas_call | solution.py:676

commit v5 on v4

--- a/solution.py
+++ b/solution.py
@@ -348,15 +348,15 @@
         for h in range(groups[p][0], groups[p][1]):
             phi_b(h)
         rs_step(1, p, 1)
+        if p == 2:
+            xgather(0, 2)
     pass_word(1)
-    xgather(0, 2)
+    xgather(1, 2)
     for p in range(PARTS):
         rs_step(1, p, 2)
-    xgather(1, 2)
     pass_word(2)
-    for step in range(3, far + 1):
-        for p in range(PARTS):
-            rs_step(1, p, step)
+    for p in range(PARTS):
+        rs_step(1, p, 3)
     for i in range(2):
         sx[i, 0, 2].wait_recv()
         sx[i, 1, 2].wait_recv()
@@ -366,6 +366,7 @@
     for p in range(PARTS):
         for h in range(groups[p][0], groups[p][1]):
             phi_a(h)
+        rs_step(1, p, far)
         rs_step(0, p, 1)
     pass_word(3)
     cts = [(RATE * v).astype(BF16) for v in rs_total(1, range(PARTS))]

time: 114 us -> 115 us (level)
    pallas_call x1, Pallas kernels: 110 us -> 112 us  [run(): pl.pallas_call(functools.partial(main_kernel, nz, n_dp // NX, n_dp), out_...]
where the time goes in v5:
time: 115 us
  Pallas kernels  114 us (99%)
    pallas_call x1, Pallas kernels, run(): pl.pallas_call(functools.partial(main_kernel, nz, n_dp // NX, n_dp), out_...  112 us
    pallas_call x1, Pallas kernels, run(): pl.pallas_call(land_kernel, out_shape=(jax.ShapeDtypeStruct(flat, BF16),...  2.32 us

profile of v5, /device:TPU:1, one launch (start us, length us, event | category | flops | bytes accessed | tf_op | source)
XLA Modules:
  0.0 115.1 jit_solution(2335385281441331952)
XLA Ops:
  0.6 112.1 %ttt_ring.1 = (bf16[128,2560]{1,0:T(8,128)(2,1)}, bf16[128,2560]{1,0:T(8,128)(2,1)}, f32[3,20,8,128]{3,2,1,0:T(8,128)}) custom-call(bf16[128,2560]{1,0:T(8,128)(2,1)} %bitcast.7, bf16[128,2560]{1,0:T(8,128)(2,1)} %bitcast.8, bf16[128,2560]{1,0:T(8,128)(2,1)} %bitcast.9, bf16[128,2560]{1,0:T(8,128)(2,1)} %bitcast.10, f32[3,20,8,128]{3,2,1,0:T(8,128)} %start.1, ...), custom_call_target="tpu_custom_call" | custom-call | tf_op jit(solution)/shard_map/ttt_ring/pallas_call | solution.py:631
  112.8 2.3 %land.1 = (bf16[128,2560]{1,0:T(8,128)(2,1)}, bf16[128,2560]{1,0:T(8,128)(2,1)}, f32[3,20,8,128]{3,2,1,0:T(8,128)}) custom-call(bf16[128,2560]{1,0:T(8,128)(2,1)} %get-tuple-element.9.dk, bf16[128,2560]{1,0:T(8,128)(2,1)} %get-tuple-element.10.dv, f32[3,20,8,128]{3,2,1,0:T(8,128)} %get-tuple-element.11.gs), custom_call_target="tpu_custom_call" | custom-call | tf_op jit(solution)/shard_map/land/pallas_call | solution.py:677
